TPU v7x, 256 devices: a whole 4x4x8 slice. The times are simulated.
256 devices in a mesh: vocab: 8 (over x_lo, y), ctx: 32 (over z, x_hi, core).
Axes of the slice: x: 4 (x_hi: 2, x_lo: 2; x = x_hi * 2 + x_lo), y: 4, z: 8, core: 2. Of those that a mesh axis runs over, the one named last changes fastest.
Arguments:
- hidden: bfloat16 [4096, 8192], P('ctx', 'vocab'), may hold values from -20 to 20
- norm_gain: float32 [8192], replicated, may hold values from 0.5 to 1.5
- head_weight: bfloat16 [152064, 8192], P(('vocab', 'ctx')), may hold values from -16 to 16
- targets: int32 [256], replicated, may hold values from 0 to 152063
- loss_rows: int32 [256], replicated, may hold values from 0 to 127, as said below
- stretch_of_slot: int32 [64], replicated, may hold values from 0 to 63, as said below
- queries: bfloat16 [4096, 8192], P('ctx', 'vocab'), may hold values from -20 to 20
- key_states: bfloat16 [4096, 1024], P('ctx', 'vocab'), may hold values from -20 to 20
- attention_values: bfloat16 [4096, 1024], P('ctx', 'vocab'), may hold values from -6 to 6
- output_weight: bfloat16 [8192, 8192], P('vocab', 'ctx'), may hold values from -0.0625 to 0.0625
Outputs:
- mean_loss: float32 [], replicated
- query_grad: bfloat16 [256, 8192], P('ctx', 'vocab')
- key_gradient: bfloat16 [4096, 1024], P('ctx', 'vocab')
- value_gradient: bfloat16 [4096, 1024], P('ctx', 'vocab')
- resid_grad: bfloat16 [8192, 256], P('ctx')
Inputs may be any that keep to these rules, and one draw needn't show every extreme that they name: `loss_rows`: within each block of 8 entries, entry j lies in rows j * 16 to (j + 1) * 16 - 1. `stretch_of_slot`: A permutation of the stretches in which slots 2c and 2c+1 hold stretches that sum to 63.
All inputs are finite; a program needn't handle non-finite values.
Results may differ from a plain program's by a relative error of at most 0.023.
Values may be sent and summed in bfloat16 or wider, within the bound.
A program may use at most 64 MiB of HBM per device.

v0:
```python
import jax
import jax.numpy as jnp
from jax import lax
from jax.sharding import PartitionSpec as P

HEAD_SIZE = 128


norm_eps = 1e-06
grad_weight = 16.0
masked_fill = -1e30


def lookup_small(indices, table):
    span = table.shape[0]
    match = indices[:, None] == lax.broadcasted_iota(jnp.int32, (1, span), 1)
    return jnp.sum(jnp.where(match, table[None, :], 0), axis=1)


def head_scores(query_heads, key_heads, query_pos, key_pos, score_scale):
    scores = (
        jnp.einsum("tjgd,sjd->jgts", query_heads, key_heads, preferred_element_type=jnp.float32)
        * score_scale
    )
    visible = key_pos[None, None, None, :] <= query_pos[None, None, :, None]
    return (jnp.where(visible, scores, masked_fill), visible)


def score_backward(prob_full, output, value_heads, grad_heads):
    row_delta = jnp.sum(
        output * jnp.transpose(grad_heads, (1, 2, 0, 3)).astype(jnp.float32), axis=3
    )
    prob_grad = jnp.einsum(
        "tjgd,sjd->jgts", grad_heads, value_heads, preferred_element_type=jnp.float32
    )
    score_grad = (prob_full * (prob_grad - row_delta[..., None])).astype(jnp.bfloat16)
    return (prob_full.astype(jnp.bfloat16), score_grad)


def per_device(
    hidden,
    norm_gain,
    head_weight,
    targets,
    loss_rows,
    stretch_of_slot,
    queries,
    key_states,
    attention_values,
    output_weight,
):
    ctx_count = lax.axis_size("ctx")
    ctx_index = lax.axis_index("ctx")
    vocab_index = lax.axis_index("vocab")
    device_rows = hidden.shape[0]
    stretch_len = device_rows // 2
    loss_total = loss_rows.shape[0]
    loss_per_device = loss_total // ctx_count
    model_width = norm_gain.shape[0]
    voc_rows = head_weight.shape[0]
    head_dim = HEAD_SIZE
    query_width = queries.shape[1]
    key_width = key_states.shape[1]
    key_head_count = key_width // head_dim
    query_group_size = query_width // key_width
    score_scale = head_dim ** (-0.5)
    cols_ctx = model_width // ctx_count
    own_rows = lax.dynamic_slice_in_dim(loss_rows, ctx_index * loss_per_device, loss_per_device)
    picked = jnp.take(hidden, own_rows, axis=0)
    wide_rows = lax.all_gather(picked, "vocab", axis=1, tiled=True)
    rows_all = lax.all_gather(wide_rows, "ctx", axis=0, tiled=True)
    rows_float = rows_all.astype(jnp.float32)
    inv_rms = lax.rsqrt(jnp.mean(rows_float * rows_float, axis=1) + norm_eps)
    normed = (rows_float * inv_rms[:, None] * norm_gain[None, :]).astype(jnp.bfloat16)
    logit_rows = lax.dot_general(
        head_weight, normed, (((1,), (1,)), ((), ())), preferred_element_type=jnp.float32
    )
    first_vocab = (vocab_index * ctx_count + ctx_index) * voc_rows
    vocab_ids = first_vocab + lax.broadcasted_iota(jnp.int32, (voc_rows, 1), 0)
    is_target = vocab_ids == targets[None, :]
    local_top = jnp.max(logit_rows, axis=0)
    target_part = jnp.sum(jnp.where(is_target, logit_rows, 0.0), axis=0)
    top_score = lax.pmax(local_top, ("vocab", "ctx"))
    local_total = jnp.sum(jnp.exp(logit_rows - top_score[None, :]), axis=0)
    row_total, target_logit = lax.psum((local_total, target_part), ("vocab", "ctx"))
    log_total = top_score + jnp.log(row_total)
    mean_loss = jnp.mean(log_total - target_logit)
    logit_grad = (
        grad_weight * (jnp.exp(logit_rows - log_total[None, :]) - is_target.astype(jnp.float32))
    ).astype(jnp.bfloat16)
    partial_rows = lax.psum_scatter(
        lax.dot_general(
            head_weight, logit_grad, (((0,), (0,)), ((), ())), preferred_element_type=jnp.float32
        ),
        "ctx",
        scatter_dimension=0,
        tiled=True,
    )
    normed_grad = lax.psum(partial_rows, "vocab")
    col_start = ctx_index * cols_ctx
    gain_part = lax.dynamic_slice_in_dim(norm_gain, col_start, cols_ctx)
    unit_rows = (lax.dynamic_slice_in_dim(rows_float, col_start, cols_ctx, 1) * inv_rms[:, None]).T
    scaled = normed_grad * gain_part[:, None]
    inner = lax.psum(jnp.sum(scaled * unit_rows, axis=0), "ctx")
    resid_grad = (inv_rms[None, :] * (scaled - unit_rows * (inner / model_width)[None, :])).astype(
        jnp.bfloat16
    )
    own_stretches = lax.dynamic_slice_in_dim(stretch_of_slot, 2 * ctx_index, 2)
    stretch_iota = lax.broadcasted_iota(jnp.int32, (1, stretch_len), 1)
    own_pos = (own_stretches[:, None] * stretch_len + stretch_iota).reshape(device_rows)
    query_mine = jnp.take(queries, own_rows, axis=0)
    attn_grad = lax.psum_scatter(
        lax.dot_general(
            resid_grad, output_weight, (((0,), (1,)), ((), ())), preferred_element_type=jnp.float32
        ),
        "ctx",
        scatter_dimension=0,
        tiled=True,
    ).astype(jnp.bfloat16)
    keys_all, value_rows_full = (
        lax.all_gather(key_states, "ctx", axis=0, tiled=True),
        lax.all_gather(attention_values, "ctx", axis=0, tiled=True),
    )
    query_heads = query_mine.reshape(loss_per_device, key_head_count, query_group_size, head_dim)
    grad_heads = attn_grad.reshape(loss_per_device, key_head_count, query_group_size, head_dim)
    key_heads = keys_all.reshape(-1, key_head_count, head_dim)
    value_heads = value_rows_full.reshape(-1, key_head_count, head_dim)
    key_pos = (stretch_of_slot[:, None] * stretch_len + stretch_iota).reshape(-1)
    query_pos = lookup_small(own_rows, own_pos)
    masked, visible = head_scores(query_heads, key_heads, query_pos, key_pos, score_scale)
    top_row = jnp.max(masked, axis=3)
    raw_weights = jnp.where(visible, jnp.exp(masked - top_row[..., None]), 0.0)
    prob_full = raw_weights / jnp.sum(raw_weights, axis=3)[..., None]
    output = jnp.einsum(
        "jgts,sjd->jgtd",
        prob_full,
        value_heads.astype(jnp.float32),
        precision=lax.Precision.HIGHEST,
    )
    prob_half, score_grad = score_backward(prob_full, output, value_heads, grad_heads)
    query_grad = (
        jnp.einsum("jgts,sjd->tjgd", score_grad, key_heads, preferred_element_type=jnp.float32)
        * score_scale
    )
    query_grad = query_grad.reshape(loss_per_device, query_width).astype(jnp.bfloat16)
    value_term = jnp.einsum(
        "jgts,tjgd->sjd", prob_half, grad_heads, preferred_element_type=jnp.float32
    )
    key_term = (
        jnp.einsum("jgts,tjgd->sjd", score_grad, query_heads, preferred_element_type=jnp.float32)
        * score_scale
    )
    key_value_sum = lax.psum_scatter(
        jnp.concatenate(
            [
                key_term.reshape(device_rows * lax.axis_size("ctx"), key_width),
                value_term.reshape(device_rows * lax.axis_size("ctx"), key_width),
            ],
            axis=1,
        ),
        "ctx",
        scatter_dimension=0,
        tiled=True,
    )
    key_gradient = key_value_sum[:, :key_width].astype(jnp.bfloat16)
    value_gradient = key_value_sum[:, key_width:].astype(jnp.bfloat16)
    return (mean_loss, query_grad, key_gradient, value_gradient, resid_grad)


def solution(mesh):
    placed = (
        P("ctx", "vocab"),
        P(),
        P(("vocab", "ctx"), None),
        P(),
        P(),
        P(),
        P("ctx", "vocab"),
        P("ctx", "vocab"),
        P("ctx", "vocab"),
        P("vocab", "ctx"),
    )
    return jax.shard_map(
        per_device,
        mesh=mesh,
        in_specs=placed,
        out_specs=(P(), P("ctx", "vocab"), P("ctx", "vocab"), P("ctx", "vocab"), P("ctx", None)),
        check_vma=False,
    )
```

profile of v0, /device:TPU:1, one launch (start us, length us, event | category | flops | bytes accessed | tf_op | source)
XLA Modules:
  0.0 946.4 jit_solution(332799858040209657)
XLA Ops:
  8.1 1.6 gather_fusion
  9.6 1.6 gather_fusion.1
  11.3 25.2 %all_gather.12 = bf16[8,8192]{1,0:T(8,128)(2,1)} all-gather(bf16[8,1024]{1,0:T(8,128)(2,1)S(1)} %get-tuple-element.34), channel_id=1, replica_groups=mesh['vocab'=8,'ctx'=32] {'vocab'}, dimensions={1}, use_global_device_ids=true | all-gather | bytes 147456 | tf_op jit(solution)/shard_map/all_gather | solution.py:70
  36.5 95.7 %all-gather.4.cloned.1.call-done = bf16[256,8192]{1,0:T(8,128)(2,1)} async-done(((bf16[8,8192]{1,0:T(8,128)(2,1)}), bf16[256,8192]{1,0:T(8,128)(2,1)}) %all-gather.4.cloned.1.call-update) | async-done | bytes 4194320 | tf_op jit(solution)/shard_map/all_gather | solution.py:71
  132.2 3.1 multiply_reduce_fusion
  135.3 7.1 fusion.46
  142.5 74.9 %pmax.7 = f32[256]{0:T(256)S(1)} all-reduce(f32[256]{0:T(256)S(1)} %get-tuple-element.35), channel_id=1, replica_groups=mesh['vocab'=8,'ctx'=32] {'vocab','ctx'}, use_global_device_ids=true, to_apply=%region_2.4 | all-reduce | flops 256 | bytes 2048 | tf_op jit(solution)/shard_map/pmax | solution.py:83
  217.6 73.3 %all-reduce = (f32[256]{0:T(256)S(1)}, f32[256]{0:T(256)S(1)}) all-reduce(f32[256]{0:T(256)S(1)} %get-tuple-element.22, f32[256]{0:T(256)S(1)} %get-tuple-element.21), channel_id=1, replica_groups=mesh['vocab'=8,'ctx'=32] {'vocab','ctx'}, use_global_device_ids=true, to_apply=%region_4.6 | all-reduce | flops 512 | bytes 4096 | tf_op jit(solution)/shard_map/psum | solution.py:85
  291.4 10.2 %convolution_bitcast_fusion = f32[8192,256]{0,1:T(8,128)} fusion(bf16[594,8192]{1,0:T(8,128)(2,1)} %param.14, f32[256,594]{0,1:T(8,128)S(1)} %get-tuple-element.36, f32[256]{0:T(256)S(1)} %get-tuple-element.26, s32[256]{0:T(256)S(1)} %copy-done.3, s32[594]{0:T(1024)S(1)} %iota_add_fusion.1), kind=kOutput, calls=%fused_computation.2 | convolution fusion | flops 2492328960 | bytes 18733384 | tf_op jit(solution)/shard_map/dot_general | solution.py:92
  301.7 147.5 %reduce-scatter.4.cloned.1.call-done = f32[256,256]{0,1:T(8,128)} async-done(((f32[8192,256]{0,1:T(8,128)}), f32[256,256]{0,1:T(8,128)}) %reduce-scatter.4.cloned.1.call-update) | async-done | bytes 262160 | tf_op jit(solution)/shard_map/reduce_scatter | solution.py:91
  450.6 6.4 convert_element_type.51
  457.0 71.1 %all-reduce.3.cloned.1.call-done = f32[256,256]{0,1:T(8,128)} async-done(((f32[256,256]{0,1:T(8,128)}), f32[256,256]{0,1:T(8,128)}) %all-reduce.3.cloned.1.call-update) | async-done | bytes 262160 | tf_op jit(solution)/shard_map/psum | solution.py:99
  528.1 1.2 fusion.37
  529.3 70.8 %psum.31 = f32[256]{0:T(256)S(1)} all-reduce(f32[256]{0:T(256)S(1)} %fusion.37), channel_id=1, replica_groups=mesh['vocab'=8,'ctx'=32] {'ctx'}, use_global_device_ids=true, to_apply=%region_14.16 | all-reduce | flops 256 | bytes 2048 | tf_op jit(solution)/shard_map/psum | solution.py:104
  601.3 1.3 fusion.48
  604.2 9.7 %all-gather.6.cloned.1.call-done = bf16[4096,128]{1,0:T(8,128)(2,1)} async-done(((bf16[128,128]{1,0:T(8,128)(2,1)}), bf16[4096,128]{1,0:T(8,128)(2,1)}) %all-gather.6.cloned.1.call-update) | async-done | bytes 1048592 | tf_op jit(solution)/shard_map/all_gather | solution.py:121
  613.9 1.8 fusion.47
  616.4 108.7 %reduce-scatter.6.cloned.1.call-done = f32[8,1024]{1,0:T(8,128)} async-done(((f32[256,1024]{1,0:T(8,128)}), f32[8,1024]{1,0:T(8,128)}) %reduce-scatter.6.cloned.1.call-update) | async-done | bytes 32784 | tf_op jit(solution)/shard_map/reduce_scatter | solution.py:112
  725.9 1.8 convolution_bitcast_fusion.1
  727.7 81.4 %all-gather.8.cloned.1.call-done = bf16[4096,128]{1,0:T(8,128)(2,1)} async-done(((bf16[128,128]{1,0:T(8,128)(2,1)}), bf16[4096,128]{1,0:T(8,128)(2,1)}) %all-gather.8.cloned.1.call-update) | async-done | bytes 1048592 | tf_op jit(solution)/shard_map/all_gather | solution.py:122
  809.1 2.3 fusion.14
  811.5 1.8 fusion.7
  813.8 2.4 pad_maximum_fusion
  818.6 117.5 %reduce-scatter.8.cloned.1.call-done = f32[128,256]{0,1:T(8,128)} async-done(((f32[4096,256]{0,1:T(8,128)}), f32[128,256]{0,1:T(8,128)}) %reduce-scatter.8.cloned.1.call-update) | async-done | bytes 131088 | tf_op jit(solution)/shard_map/reduce_scatter | solution.py:153
  (54 shorter events, 12.0 us)
Async XLA Ops:
  7.2 594.1 %copy-start = (bf16[1024,256]{1,0:T(8,128)(2,1)S(1)}, bf16[1024,256]{1,0:T(8,128)(2,1)}, u32[]{:S(2)}) copy-start(bf16[1024,256]{1,0:T(8,128)(2,1)} %param.21) | copy-start | bytes 1572868
  7.2 125.0 %all-gather.4.cloned.1.call-start = ((), (), s32[]{:S(2)}) async-start(), calls=%async_computation.3 | async-start | bytes 4325376 | tf_op jit(solution)/shard_map/all_gather | solution.py:71
  36.5 412.7 %reduce-scatter.4.cloned.1.call-start = ((), (), s32[]{:S(2)}) async-start(), calls=%async_computation.5 | async-start | bytes 8650752 | tf_op jit(solution)/shard_map/reduce_scatter | solution.py:91
  135.3 82.1 %copy-start.3 = (s32[256]{0:T(256)S(1)}, s32[256]{0:T(256)}, u32[]{:S(2)}) copy-start(s32[256]{0:T(256)} %param.15) | copy-start | bytes 3076
  301.6 226.5 %all-reduce.3.cloned.1.call-start = ((), (), s32[]{:S(2)}) async-start(), calls=%async_computation.6 | async-start | bytes 524288 | tf_op jit(solution)/shard_map/psum | solution.py:99
  449.1 154.3 %copy-start.4 = (s32[64]{0:T(128)S(1)}, s32[64]{0:T(128)}, u32[]{:S(2)}) copy-start(s32[64]{0:T(128)} %param.17) | copy-start | bytes 772
  449.2 164.7 %all-gather.6.cloned.1.call-start = ((), (), s32[]{:S(2)}) async-start(), calls=%async_computation.4 | async-start | bytes 1081344 | tf_op jit(solution)/shard_map/all_gather | solution.py:121
  449.7 275.4 %reduce-scatter.6.cloned.1.call-start = ((), (), s32[]{:S(2)}) async-start(), calls=%async_computation.7 | async-start | bytes 1081344 | tf_op jit(solution)/shard_map/reduce_scatter | solution.py:112
  602.7 206.5 %all-gather.8.cloned.1.call-start = ((), (), s32[]{:S(2)}) async-start(), calls=%async_computation.8 | async-start | bytes 1081344 | tf_op jit(solution)/shard_map/all_gather | solution.py:122
  603.2 332.8 %reduce-scatter.8.cloned.1.call-start = ((), (), s32[]{:S(2)}) async-start(), calls=%async_computation.9 | async-start | bytes 4325376 | tf_op jit(solution)/shard_map/reduce_scatter | solution.py:153
  809.1 4.7 copy-start.1
  813.2 4.4 copy-start.2
Sparse Core Ops, SparseCore 0:
  36.6 95.5 all-gather.3
  301.7 147.3 reduce-scatter.3
  451.8 76.2 all-reduce.2
  530.7 83.1 all-gather.5
  617.8 107.2 reduce-scatter.5
  727.8 81.3 all-gather.7
  816.4 119.6 reduce-scatter.7
where the time goes:
time: 951 us; the launch traced here: 946 us
  waiting for transfers between devices  633 us (67%)
  blocking collectives  244 us (26%)
  matrix products  27.2 us (3%)
  other arithmetic  18.9 us (2%)
  between operations  16.1 us (2%)
    reduce_scatter x1, waiting for transfers between devices, per_device(): lax.psum_scatter(lax.dot_general(head_weight, logit_grad, (((0,), (0,)),...  147 us
    reduce_scatter x1, waiting for transfers between devices, per_device(): lax.psum_scatter(jnp.concatenate([key_term.reshape(device_rows * lax.axis...  117 us
    reduce_scatter x1, waiting for transfers between devices, per_device(): lax.psum_scatter(lax.dot_general(resid_grad, output_weight, (((0,), (1,))...  109 us
    all_gather x1, waiting for transfers between devices, per_device(): rows_all = lax.all_gather(wide_rows, 'ctx', axis=0, tiled=True)  95.7 us
    all_gather x1, waiting for transfers between devices, per_device(): lax.all_gather(attention_values, 'ctx', axis=0, tiled=True)  81.4 us
    pmax x1, blocking collectives, per_device(): top_score = lax.pmax(local_top, ('vocab', 'ctx'))  74.9 us
    psum x1, blocking collectives, per_device(): lax.psum((local_total, target_part), ('vocab', 'ctx'))  73.3 us
    psum x1, waiting for transfers between devices, per_device(): normed_grad = lax.psum(partial_rows, 'vocab')  71.1 us
  transfers between devices with their start and end apart: 7, of which 7 were waited for; matrix products, arithmetic and copies ran while one was open for 2% of the time, Pallas kernels for 0%

commit v1 on v0

v1 whole, which is shorter than its diff:
```python
import functools

import jax
import jax.numpy as jnp
from jax import lax
from jax.experimental import pallas as pl
from jax.experimental.pallas import tpu as pltpu
from jax.sharding import PartitionSpec as P

MESH = pl.DeviceIdType.MESH
F32 = jnp.float32
BF16 = jnp.bfloat16

HEAD = 128
ROWS = 256
WIDTH = 8192
NV, NC, NZ = 8, 32, 8
LPD = 8
VOC = 594
PAD = 640
KVQ = 320
EPS = 1e-06
GRAD_WEIGHT = 16.0
SCALE = HEAD ** (-0.5)
FILL = -1e30

ORDERS = (
    (("x", 1), ("x", 3), ("y", 1), ("y", 3)),
    (("x", 3), ("x", 1), ("y", 3), ("y", 1)),
    (("y", 1), ("y", 3), ("x", 1), ("x", 3)),
    (("y", 3), ("y", 1), ("x", 3), ("x", 1)),
)


class Place:
    def __init__(self):
        self.v = lax.axis_index("vocab")
        self.c = lax.axis_index("ctx")
        self.xl = lax.div(self.v, 4)
        self.y = lax.rem(self.v, 4)
        self.z = lax.div(self.c, 4)
        self.xh = lax.rem(lax.div(self.c, 2), 2)
        self.core = lax.rem(self.c, 2)

    def y_off(self, off):
        y = self.y
        if off == 0:
            return y
        if off == 1:
            return y + 1 - 2 * lax.rem(y, 2)
        if off == 2:
            return lax.rem(y + 2, 4)
        return 3 - y

    def xl_off(self, off):
        return 1 - self.xl if off & 1 else self.xl

    def xh_off(self, off):
        return 1 - self.xh if off & 2 else self.xh

    def v_at(self, x_off=0, y_off=0):
        return self.xl_off(x_off) * 4 + self.y_off(y_off)

    def dev(self, x_off=0, y_off=0, z=None, core_off=0):
        z = self.z if z is None else z
        core = 1 - self.core if core_off else self.core
        return (self.v_at(x_off, y_off), z * 4 + self.xh_off(x_off) * 2 + core)

    def z_plus(self, d):
        return lax.rem(self.z + d + NZ, NZ)


def greet(devices):
    barrier = pltpu.get_barrier_semaphore()
    for device in devices:
        pl.semaphore_signal(barrier, inc=1, device_id=device, device_id_type=MESH)
    return functools.partial(pl.semaphore_wait, barrier, len(devices))


def remote(src, dst, send, recv, device):
    copy = pltpu.make_async_remote_copy(
        src_ref=src, dst_ref=dst, send_sem=send, recv_sem=recv, device_id=device, device_id_type=MESH
    )
    copy.start()
    return copy


def offsets(order, done):
    held = [(0, 0)]
    for axis, mask in order[:done]:
        held = held + [(ox ^ mask, oy) if axis == "x" else (ox, oy ^ mask) for ox, oy in held]
    return held


def partner(me, axis, mask):
    return me.dev(x_off=mask) if axis == "x" else me.dev(y_off=mask)


def gather_kernel(
    hidden, queries, keys, values, lrows, rows, kvq, z_s, z_r, a_s, a_r, f_s, f_r, k_s, k_r, kf_s, kf_r
):
    me = Place()
    mate = me.dev(core_off=1)
    greeted = greet(
        [me.dev(z=me.z_plus(d)) for d in range(1, NZ)]
        + [me.dev(x_off=1), me.dev(x_off=2), me.dev(x_off=3), me.dev(y_off=1), me.dev(y_off=3), mate]
    )
    own = lrows[me.c]
    pick = (own == lax.broadcasted_iota(jnp.int32, (LPD, hidden.shape[0]), 1)).astype(F32).astype(BF16)
    mine_cols = pl.ds(pl.multiple_of(me.v * 1024, 1024), 1024)
    rows[me.z, me.xh, me.core, :, mine_cols] = jnp.dot(
        pick, hidden[...], preferred_element_type=F32
    ).astype(BF16)
    picked_q = jnp.dot(pick, queries[...], preferred_element_type=F32).astype(BF16)
    kvq[me.z, me.xh, me.core, 0:128, :] = keys[...]
    kvq[me.z, me.xh, me.core, 128:256, :] = values[...]
    for head in range(8):
        kvq[me.z, me.xh, me.core, 256 + 8 * head : 264 + 8 * head, :] = picked_q[:, 128 * head : 128 * head + 128]
    greeted()
    started = []

    def go(*args):
        copy = remote(*args)
        started.append(copy)
        return copy

    def block(k, off):
        cols = pl.ds(pl.multiple_of(me.v_at(*off) * 1024, 1024), 1024)
        return rows.at[pl.ds(2 * k, 2), me.xh_off(off[0]), me.core, :, cols]

    own_block = rows.at[me.z, me.xh, me.core, :, mine_cols]
    z_copies = [
        go(own_block, own_block, z_s.at[d], z_r.at[d], me.dev(z=me.z_plus(d))) for d in range(1, NZ)
    ]
    own_kvq = kvq.at[me.z, me.xh, me.core]
    k_x = go(own_kvq, own_kvq, k_s.at[0], k_r.at[0], me.dev(x_off=2))
    for copy in z_copies:
        copy.wait_recv()

    a_copies = {}

    def a_step(step):
        for k, order in enumerate(ORDERS):
            axis, mask = order[step]
            for j, off in enumerate(offsets(order, step)):
                slot = (1 << step) - 1 + j
                here = block(k, off)
                a_copies[k, step, j] = go(
                    here, here, a_s.at[k, slot], a_r.at[k, slot], partner(me, axis, mask)
                )

    def forward(k, j, off):
        here = block(k, off)
        f_copies.append(go(here, here, f_s.at[k, j], f_r.at[k, j], mate))

    def a_wait(step):
        count = 1 << step
        for j in range(count):
            for k, order in enumerate(ORDERS):
                a_copies[k, step, j].wait_recv()
                forward(k, count + j, offsets(order, step + 1)[count + j])

    f_copies, kf_copies, ring = [], [], {}

    def ring_step(step):
        lo, hi = (0, KVQ) if step < 4 else (0, 160)
        lo2, hi2 = (0, KVQ) if step < 4 else (160, KVQ)
        up, down = me.z_plus(-(step - 1)), me.z_plus(step - 1)
        right = kvq.at[up, :, me.core, lo:hi]
        left = kvq.at[down, :, me.core, lo2:hi2]
        ring[step] = (
            go(right, right, k_s.at[2 * step - 1], k_r.at[2 * step - 1], me.dev(z=me.z_plus(1))),
            go(left, left, k_s.at[2 * step], k_r.at[2 * step], me.dev(z=me.z_plus(-1))),
        )

    def ring_forward(slot, z):
        here = kvq.at[z, :, me.core]
        kf_copies.append(go(here, here, kf_s.at[slot], kf_r.at[slot], mate))

    def ring_wait(step):
        ring[step][0].wait_recv()
        if step < 4:
            ring_forward(2 * step - 1, me.z_plus(-step))
        ring[step][1].wait_recv()
        ring_forward(2 * step if step < 4 else 7, me.z_plus(step))

    a_step(0)
    for k in range(4):
        forward(k, 0, (0, 0))
    k_x.wait_recv()
    ring_step(1)
    ring_forward(0, me.z)
    a_wait(0)
    a_step(1)
    a_wait(1)
    a_step(2)
    ring_wait(1)
    ring_step(2)
    a_wait(2)
    a_step(3)
    ring_wait(2)
    ring_step(3)
    a_wait(3)
    ring_wait(3)
    ring_step(4)
    ring_wait(4)
    for copy in f_copies + kf_copies:
        copy.wait_recv()
    for copy in started:
        copy.wait_send()


def gather(hidden, queries, keys, values, lrows):
    vmem = pl.BlockSpec(memory_space=pltpu.VMEM)
    dma = pltpu.SemaphoreType.DMA
    return pl.pallas_call(
        gather_kernel,
        out_shape=(
            jax.ShapeDtypeStruct((NZ, 2, 2, LPD, WIDTH), BF16),
            jax.ShapeDtypeStruct((NZ, 2, 2, KVQ, HEAD), BF16),
        ),
        in_specs=[vmem] * 5,
        out_specs=(vmem, vmem),
        scratch_shapes=[
            dma((NZ,)), dma((NZ,)), dma((4, 15)), dma((4, 15)), dma((4, 16)), dma((4, 16)),
            dma((9,)), dma((9,)), dma((8,)), dma((8,)),
        ],
        compiler_params=pltpu.CompilerParams(collective_id=0, has_side_effects=True),
        name="gather",
    )(hidden, queries, keys, values, lrows)


def column(row_vector, width=128):
    return jnp.transpose(jnp.broadcast_to(row_vector, (width, row_vector.shape[1])))


def merge(parts):
    top = jnp.max(parts[:, 0:2], axis=0)
    weight = jnp.exp(parts[:, 0:2] - top[None])
    total = jnp.sum(parts[:, 2:4] * weight, axis=0)
    first = jnp.sum(parts[:, 4:6] * weight, axis=0)
    hit = jnp.sum(parts[:, 6:8], axis=0)
    return jnp.concatenate([top, total, first, hit], axis=0)


def wide(two):
    return jnp.concatenate([two[0:1], two[1:2]], axis=1)


def loss_kernel(
    rows, gain, targets, weight_hbm, loss, resid_t, resid,
    weight, y, logits, grad_t, rms_col, inner_col, st1, st2, cs, cr, acc, sb1, sb2, sb3, sb4, rb1, rb2, rb3, rb4,
    zs, zr, w_sem, s1_s, s1_r, s2_s, s2_r, c_s, c_r, x_s, x_r, z_s, z_r, v_s, v_r,
):
    me = Place()
    mate = me.dev(core_off=1)
    group1 = [(d, o) for d in range(NZ) for o in range(2) if (d, o) != (0, 0)]
    group2 = [(ox, oy) for ox in range(4) for oy in range(4) if (ox, oy) != (0, 0)]
    greeted = greet(
        [me.dev(z=me.z_plus(d), core_off=o) for d, o in group1] + [me.dev(ox, oy) for ox, oy in group2]
    )
    loads = []
    for j in range(8):
        part = (slice(None), slice(1024 * j, 1024 * j + 1024))
        load = pltpu.make_async_copy(weight_hbm.at[part], weight.at[part], w_sem.at[j])
        load.start()
        loads.append(load)

    def prepare(j, square):
        cols = pl.ds(pl.multiple_of(j * 1024, 1024), 1024)
        x = rows[:, :, :, :, cols].astype(F32).reshape(ROWS, 1024)
        y[:, cols] = (x * gain[:, cols]).astype(BF16)
        sq = x * x
        for t in range(8):
            square = square + sq[:, 128 * t : 128 * t + 128]
        return square

    square = lax.fori_loop(0, 8, prepare, jnp.zeros((ROWS, 128), F32))
    inv_col = lax.rsqrt(jnp.sum(square, axis=1, keepdims=True) * (1.0 / WIDTH) + EPS)
    rms_col[...] = jnp.broadcast_to(inv_col, (ROWS, 128))
    inv_row = jnp.transpose(rms_col[...])[0:1, :]

    logits[PAD - 48 : PAD, :] = jnp.zeros((48, ROWS), F32)
    for j in range(8):
        loads[j].wait()
        term = lax.dot_general(
            weight[:, 1024 * j : 1024 * j + 1024], y[:, 1024 * j : 1024 * j + 1024],
            (((1,), (1,)), ((), ())), preferred_element_type=F32,
        )
        logits[0:VOC, :] = term if j == 0 else logits[0:VOC, :] + term

    ids = lax.broadcasted_iota(jnp.int32, (PAD, ROWS), 0)
    real = ids < VOC
    first_id = (me.v * NC + me.c) * VOC
    is_target = ((ids + first_id) == targets[...]) & real
    value = jnp.where(real, logits[...] * inv_row, FILL)
    logits[...] = value
    top = jnp.max(value, axis=0, keepdims=True)
    raw = jnp.exp(value - top)
    stats = (
        top,
        jnp.sum(raw, axis=0, keepdims=True),
        jnp.sum(raw * value, axis=0, keepdims=True),
        jnp.sum(jnp.where(is_target, value, 0.0), axis=0, keepdims=True),
    )
    packed = jnp.concatenate([part[:, h : h + 128] for part in stats for h in (0, 128)], axis=0)
    greeted()
    started = []

    def go(*args):
        copy = remote(*args)
        started.append(copy)
        return copy

    slot1 = me.z * 2 + me.core
    st1[slot1] = packed
    waits = []
    for i, (d, o) in enumerate(group1):
        waits.append(
            go(st1.at[slot1], st1.at[slot1], s1_s.at[i], s1_r.at[2 * d + o], me.dev(z=me.z_plus(d), core_off=o))
        )
    for copy in waits:
        copy.wait_recv()
    slot2 = (me.xh * 2 + me.xl) * 4 + me.y
    st2[slot2] = merge(st1[...])
    waits = []
    for i, (ox, oy) in enumerate(group2):
        waits.append(go(st2.at[slot2], st2.at[slot2], s2_s.at[i], s2_r.at[4 * ox + oy], me.dev(ox, oy)))
    for copy in waits:
        copy.wait_recv()
    final = merge(st2[...])
    log_total = wide(final[0:2] + jnp.log(final[2:4]))
    hit = wide(final[6:8])
    loss[...] = jnp.broadcast_to(jnp.mean(log_total - hit, axis=1, keepdims=True), (8, 128))
    inner = (wide(final[4:6] / final[2:4]) - hit) * (GRAD_WEIGHT / WIDTH)
    inner_col[...] = column(inner)
    grad = GRAD_WEIGHT * (jnp.exp(logits[...] - log_total) - is_target.astype(F32))
    grad_t[...] = jnp.transpose(grad).astype(BF16)

    def chunk(z, xh, core):
        cols = pl.ds(pl.multiple_of((z * 4 + xh * 2 + core) * 256, 256), 256)
        return jnp.dot(grad_t[:, 0:VOC], weight[:, cols], preferred_element_type=F32).reshape(NV, 32, 256)

    c_copies = []
    for k in range(4):

        def other(i, _):
            z, xh = 2 * k + lax.div(i, 2), lax.rem(i, 2)
            cs[z, xh] = chunk(z, xh, 1 - me.core).astype(BF16)
            return 0

        lax.fori_loop(0, 4, other, 0)
        part = pl.ds(2 * k, 2)
        c_copies.append(go(cs.at[part], cr.at[part], c_s.at[k], c_r.at[k], mate))

    def own(i, _):
        z, xh = lax.div(i, 2), lax.rem(i, 2)
        acc[z, xh] = chunk(z, xh, me.core)
        return 0

    lax.fori_loop(0, 16, own, 0)

    sends, recvs = (sb1, sb2, sb3, sb4), (rb1, rb2, rb3, rb4)
    moving = {}

    def at(z, off):
        return (z, me.xh_off(off[0]), me.v_at(*off))

    for step in range(4):
        for k in range(4):
            order = ORDERS[k][::-1]
            back = ORDERS[k]
            axis, mask = order[step]
            keep = offsets(back, 3 - step)
            if step == 0:
                c_copies[k].wait_recv()
            else:
                moving[k, step - 1].wait_recv()
            before = offsets(back, 4 - step)
            for z2 in range(2):
                z = 2 * k + z2
                for off in before:
                    here = at(z, off)
                    if step == 0:
                        extra = cr[here].astype(F32)
                    else:
                        extra = recvs[step - 1][k, z2, before.index(off)].astype(F32)
                    summed = acc[here] + extra
                    away = (off[0] ^ mask, off[1]) if axis == "x" else (off[0], off[1] ^ mask)
                    if away in keep:
                        sends[step][k, z2, keep.index(away)] = summed.astype(BF16)
                    else:
                        acc[here] = summed
            moving[k, step] = go(
                sends[step].at[k], recvs[step].at[k], x_s.at[k, step], x_r.at[k, step], partner(me, axis, mask)
            )
    for k in range(4):
        moving[k, 3].wait_recv()
        for z2 in range(2):
            z = 2 * k + z2
            here = at(z, (0, 0))
            summed = acc[here] + rb4[k, z2, 0].astype(F32)
            acc[here] = summed
            zs[z] = summed.astype(BF16)
    z_copies = []
    for d in range(1, NZ):
        z = me.z_plus(d)
        z_copies.append(go(zs.at[z], zr.at[me.z], z_s.at[d], z_r.at[d], me.dev(z=z)))
    zr[me.z] = zs[me.z]
    for copy in z_copies:
        copy.wait_recv()
    normed_grad = jnp.sum(zr[...].astype(F32), axis=0)
    cols = pl.ds(pl.multiple_of(me.c * 256, 256), 256)
    lines = pl.ds(pl.multiple_of(me.v * 32, 32), 32)
    inv = rms_col[lines, 0:1]
    picked = rows[me.v, :, :, :, cols].astype(F32).reshape(32, 256)
    out = inv * (normed_grad * gain[:, cols] - picked * (inv * inner_col[lines, 0:1]))
    resid[me.v] = out.astype(BF16)
    v_copies = []
    for i, (ox, oy) in enumerate([(o, q) for o in range(2) for q in range(4) if (o, q) != (0, 0)]):
        v_copies.append(go(resid.at[me.v], resid.at[me.v], v_s.at[i], v_r.at[i], me.dev(ox, oy)))
    for copy in v_copies:
        copy.wait_recv()
    resid_t[...] = jnp.transpose(resid[...].astype(F32).reshape(ROWS, 256)).astype(BF16)
    for copy in started:
        copy.wait_send()


def loss_part(rows, gain, targets, head_weight):
    vmem = pl.BlockSpec(memory_space=pltpu.VMEM)
    dma = pltpu.SemaphoreType.DMA
    scratch = pltpu.VMEM
    halves = [8, 4, 2, 1]
    return pl.pallas_call(
        loss_kernel,
        out_shape=(
            jax.ShapeDtypeStruct((8, 128), F32),
            jax.ShapeDtypeStruct((256, ROWS), BF16),
            jax.ShapeDtypeStruct((NV, 32, 256), BF16),
        ),
        in_specs=[vmem, vmem, vmem, pl.BlockSpec(memory_space=pl.ANY)],
        out_specs=(vmem, vmem, vmem),
        scratch_shapes=[
            scratch((VOC, WIDTH), BF16),
            scratch((ROWS, WIDTH), BF16),
            scratch((PAD, ROWS), F32),
            scratch((ROWS, PAD), BF16),
            scratch((ROWS, 128), F32),
            scratch((ROWS, 128), F32),
            scratch((16, 8, 128), F32),
            scratch((16, 8, 128), F32),
            scratch((NZ, 2, NV, 32, 256), BF16),
            scratch((NZ, 2, NV, 32, 256), BF16),
            scratch((NZ, 2, NV, 32, 256), F32),
            *[scratch((4, 2, n, 32, 256), BF16) for n in halves],
            *[scratch((4, 2, n, 32, 256), BF16) for n in halves],
            scratch((NZ, 32, 256), BF16),
            scratch((NZ, 32, 256), BF16),
            dma((8,)),
            dma((16,)), dma((16,)), dma((16,)), dma((16,)), dma((4,)), dma((4,)),
            dma((4, 4)), dma((4, 4)), dma((NZ,)), dma((NZ,)), dma((7,)), dma((7,)),
        ],
        compiler_params=pltpu.CompilerParams(
            collective_id=1, has_side_effects=True, vmem_limit_bytes=60 * 1024 * 1024
        ),
        name="loss_part",
    )(rows, gain, targets, head_weight)


def attention_kernel(
    resid, out_weight, kvq, key_pos, query_pos, key_col, query_col, dq, dk, dv,
    k_all, v_all, probs, part, cr, acc, rs, rr, grads, extras, st, s2, q_all,
    c_s, c_r, r_s, r_r, g_s, g_r, e_s, e_r, fg_s, fg_r, fe_s, fe_r,
):
    me = Place()
    mate = me.dev(core_off=1)
    peers = [(d, o) for d in range(NZ) for o in (0, 2) if (d, o) != (0, 0)]
    greeted = greet([me.dev(z=me.z_plus(d), x_off=o) for d, o in peers] + [mate])
    started = []

    def go(*args):
        copy = remote(*args)
        started.append(copy)
        return copy

    wide_part = lax.dot_general(
        resid[...].reshape(ROWS, 256), out_weight[...], (((1,), (1,)), ((), ())), preferred_element_type=F32
    )
    for h in range(8):
        part[:, :, :, 8 * h : 8 * h + 8, :] = wide_part[:, 128 * h : 128 * h + 128].reshape(NZ, 2, 2, LPD, HEAD)
    cs = acc
    cs[...] = part[:, :, 1 - me.core].astype(BF16)
    greeted()
    c_copy = go(cs, cr, c_s, c_r, mate)

    k_all[...] = kvq[:, :, :, 0:128, :].reshape(NC * 128, HEAD)
    v_all[...] = kvq[:, :, :, 128:256, :].reshape(NC * 128, HEAD)
    q_all[...] = kvq[:, :, :, 256:320, :].reshape(NC * 64, HEAD)
    q_own = kvq[me.z, me.xh, me.core, 256:320, :]
    c_copy.wait_recv()
    rs[...] = (part[:, :, me.core] + cr[...].astype(F32)).astype(BF16)
    r_copies = []
    for i, (d, o) in enumerate(peers):
        z, xh = me.z_plus(d), me.xh_off(o)
        r_copies.append(
            go(rs.at[z, xh], rr.at[me.z, me.xh], r_s.at[i], r_r.at[i], me.dev(z=z, x_off=o))
        )
    rr[me.z, me.xh] = rs[me.z, me.xh]
    scores = lax.dot_general(q_own, k_all[...], (((1,), (1,)), ((), ())), preferred_element_type=F32)
    seen = key_pos[...] <= query_col[...]
    masked = jnp.where(seen, scores * SCALE, FILL)
    top = jnp.max(masked, axis=1, keepdims=True)
    raw = jnp.where(seen, jnp.exp(masked - top), 0.0)
    total = jnp.sum(raw, axis=1, keepdims=True)
    probs[...] = raw / total
    log_total = top + jnp.log(total)
    high = probs[...].astype(BF16)
    low = (probs[...] - high.astype(F32)).astype(BF16)
    out = jnp.dot(high, v_all[...], preferred_element_type=F32) + jnp.dot(
        low, v_all[...], preferred_element_type=F32
    )
    k_own = kvq[me.z, me.xh, me.core, 0:128, :]
    v_own = kvq[me.z, me.xh, me.core, 128:256, :]
    s2[...] = lax.dot_general(k_own, q_all[...], (((1,), (1,)), ((), ())), preferred_element_type=F32)
    for copy in r_copies:
        copy.wait_recv()
    grad_own = jnp.sum(rr[...].astype(F32), axis=(0, 1)).astype(BF16)
    grads[me.z, me.xh, me.core] = grad_own
    delta = jnp.sum(grad_own.astype(F32) * out, axis=1, keepdims=True)
    lane = lax.broadcasted_iota(jnp.int32, (64, 128), 1)
    both = jnp.where(lane == 0, delta, jnp.where(lane == 1, log_total, 0.0))
    st[...] = jnp.zeros((128, 128), F32)
    st[0:64, :] = both
    extras[me.z, me.xh, me.core] = jnp.transpose(st[...])[0:8, :]
    own_g, own_e = grads.at[me.z, me.xh, me.core], extras.at[me.z, me.xh, me.core]
    g_copies = []
    for i, (d, o) in enumerate(peers):
        device = me.dev(z=me.z_plus(d), x_off=o)
        g_copies.append(
            (
                go(own_g, own_g, g_s.at[i], g_r.at[i], device),
                go(own_e, own_e, e_s.at[i], e_r.at[i], device),
                d,
                o,
            )
        )
    forwards = [
        go(own_g, own_g, fg_s.at[15], fg_r.at[15], mate),
        go(own_e, own_e, fe_s.at[15], fe_r.at[15], mate),
    ]
    prob_grad = lax.dot_general(grad_own, v_all[...], (((1,), (1,)), ((), ())), preferred_element_type=F32)
    score_grad = (probs[...] * (prob_grad - delta)).astype(BF16)
    query_grad = (jnp.dot(score_grad, k_all[...], preferred_element_type=F32) * SCALE).astype(F32)
    for h in range(8):
        dq[:, 128 * h : 128 * h + 128] = query_grad[8 * h : 8 * h + 8, :].astype(BF16)
    for i, (g_copy, e_copy, d, o) in enumerate(g_copies):
        z, xh = me.z_plus(-d), me.xh_off(o)
        g_copy.wait_recv()
        e_copy.wait_recv()
        here_g, here_e = grads.at[z, xh, me.core], extras.at[z, xh, me.core]
        forwards.append(go(here_g, here_g, fg_s.at[i], fg_r.at[i], mate))
        forwards.append(go(here_e, here_e, fe_s.at[i], fe_r.at[i], mate))
    for copy in forwards:
        copy.wait_recv()
    grads_all = grads[...].reshape(NC * 64, HEAD)
    e_all = extras[...].reshape(NC, 8, 128)
    delta_all = jnp.concatenate([e_all[i, 0:1, 0:64] for i in range(NC)], axis=1)
    log_all = jnp.concatenate([e_all[i, 1:2, 0:64] for i in range(NC)], axis=1)
    seen2 = key_col[...] <= query_pos[...]
    probs2 = jnp.where(seen2, jnp.exp(s2[...] * SCALE - log_all), 0.0)
    dv[...] = jnp.dot(probs2.astype(BF16), grads_all, preferred_element_type=F32).astype(BF16)
    prob_grad2 = lax.dot_general(v_own, grads_all, (((1,), (1,)), ((), ())), preferred_element_type=F32)
    score_grad2 = (probs2 * (prob_grad2 - delta_all)).astype(BF16)
    dk[...] = (jnp.dot(score_grad2, q_all[...], preferred_element_type=F32) * SCALE).astype(BF16)
    for copy in started:
        copy.wait_send()


def attention_part(resid, out_weight, kvq, key_pos, query_pos, key_col, query_col):
    vmem = pl.BlockSpec(memory_space=pltpu.VMEM)
    dma = pltpu.SemaphoreType.DMA
    scratch = pltpu.VMEM
    return pl.pallas_call(
        attention_kernel,
        out_shape=(
            jax.ShapeDtypeStruct((LPD, 1024), BF16),
            jax.ShapeDtypeStruct((128, HEAD), BF16),
            jax.ShapeDtypeStruct((128, HEAD), BF16),
        ),
        in_specs=[vmem] * 7,
        out_specs=(vmem, vmem, vmem),
        scratch_shapes=[
            scratch((NC * 128, HEAD), BF16),
            scratch((NC * 128, HEAD), BF16),
            scratch((64, NC * 128), F32),
            scratch((NZ, 2, 2, 64, HEAD), F32),
            scratch((NZ, 2, 64, HEAD), BF16),
            scratch((NZ, 2, 64, HEAD), BF16),
            scratch((NZ, 2, 64, HEAD), BF16),
            scratch((NZ, 2, 64, HEAD), BF16),
            scratch((NZ, 2, 2, 64, HEAD), BF16),
            scratch((NZ, 2, 2, 8, 128), F32),
            scratch((128, 128), F32),
            scratch((128, NC * 64), F32),
            scratch((NC * 64, HEAD), BF16),
            dma, dma, dma((15,)), dma((15,)), dma((15,)), dma((15,)), dma((15,)), dma((15,)),
            dma((16,)), dma((16,)), dma((16,)), dma((16,)),
        ],
        compiler_params=pltpu.CompilerParams(
            collective_id=2, has_side_effects=True, vmem_limit_bytes=60 * 1024 * 1024
        ),
        name="attention_part",
    )(resid, out_weight, kvq, key_pos, query_pos, key_col, query_col)


def per_device(
    hidden,
    norm_gain,
    head_weight,
    targets,
    loss_rows,
    stretch_of_slot,
    queries,
    key_states,
    attention_values,
    output_weight,
):
    c = lax.axis_index("ctx")
    spans = stretch_of_slot.reshape(NC, 2)
    local = loss_rows.reshape(NC, LPD)
    place = jnp.where(local < 64, spans[:, 0:1], spans[:, 1:2]) * 64 + lax.rem(local, 64)
    query_pos = jnp.broadcast_to(place[:, None, :], (NC, 8, LPD)).reshape(1, NC * 64)
    query_col = lax.dynamic_slice_in_dim(query_pos, c * 64, 64, 1).reshape(64, 1)
    key_pos = (stretch_of_slot[:, None] * 64 + lax.broadcasted_iota(jnp.int32, (64, 64), 1)).reshape(1, 4096)
    key_col = lax.dynamic_slice_in_dim(key_pos, c * 128, 128, 1).reshape(128, 1)
    rows, kvq = gather(hidden, queries, key_states, attention_values, loss_rows.reshape(NC, LPD, 1))
    loss, resid_t, resid = loss_part(
        rows, norm_gain.reshape(1, WIDTH), targets.reshape(1, ROWS), head_weight
    )
    dq, dk, dv = attention_part(resid, output_weight, kvq, key_pos, query_pos, key_col, query_col)
    return (loss[0, 0], dq, dk, dv, resid_t)


def solution(mesh):
    placed = (
        P("ctx", "vocab"),
        P(),
        P(("vocab", "ctx"), None),
        P(),
        P(),
        P(),
        P("ctx", "vocab"),
        P("ctx", "vocab"),
        P("ctx", "vocab"),
        P("vocab", "ctx"),
    )
    return jax.shard_map(
        per_device,
        mesh=mesh,
        in_specs=placed,
        out_specs=(P(), P("ctx", "vocab"), P("ctx", "vocab"), P("ctx", "vocab"), P("ctx", None)),
        check_vma=False,
    )
```

time: 951 us -> 153 us (0.16)
  waiting for transfers between devices: 633 us -> 0 us
  blocking collectives: 244 us -> 0 us
  Pallas kernels: 0 us -> 142 us
  matrix products: 27.2 us -> 0 us
  other arithmetic: 18.9 us -> 0.15 us
  between operations: 16.1 us -> 0.75 us
    reduce_scatter x3 -> x0, waiting for transfers between devices: 374 us -> none  [the longest x1 147 us: per_device(): lax.psum_scatter(lax.dot_general(head_weight, logit_grad, (((0,), (0,)),...]
    all_gather x3 -> x0, waiting for transfers between devices: 187 us -> none  [the longest x1 95.7 us: per_device(): rows_all = lax.all_gather(wide_rows, 'ctx', axis=0, tiled=True)]
    psum x2 -> x0, blocking collectives: 144 us -> none  [the longest x1 73.3 us: per_device(): lax.psum((local_total, target_part), ('vocab', 'ctx'))]
    pallas_call x0 -> x3, Pallas kernels: none -> 142 us  [the longest x1 56.3 us: loss_part(): pl.pallas_call(loss_kernel, out_shape=(jax.ShapeDtypeStruct((8, 128), F32...]
    pmax x1 -> x0, blocking collectives: 74.9 us -> none  [per_device(): top_score = lax.pmax(local_top, ('vocab', 'ctx'))]
    psum x1 -> x0, waiting for transfers between devices: 71.1 us -> none  [per_device(): normed_grad = lax.psum(partial_rows, 'vocab')]
    dot_general x9 -> x0, matrix products: 27.2 us -> none  [the longest x1 10.2 us: per_device(): lax.dot_general(head_weight, logit_grad, (((0,), (0,)), ((), ())), prefer...]
    all_gather x1 -> x0, blocking collectives: 25.2 us -> none  [per_device(): wide_rows = lax.all_gather(picked, 'vocab', axis=1, tiled=True)]
  transfers between devices with their start and end apart: 7 -> 0, of which waited for: 7 -> 0; matrix products, arithmetic and copies ran while one was open for 2% -> 0% of each run, Pallas kernels for 0% -> 0%
where the time goes in v1:
time: 153 us
  Pallas kernels  142 us (93%)
  local copies, waits for them, and re-layouts  9.65 us (6%)
    pallas_call x1, Pallas kernels, loss_part(): pl.pallas_call(loss_kernel, out_shape=(jax.ShapeDtypeStruct((8, 128), F32...  56.3 us
    pallas_call x1, Pallas kernels, gather(): pl.pallas_call(gather_kernel, out_shape=(jax.ShapeDtypeStruct((NZ, 2, 2,...  48.6 us
    pallas_call x1, Pallas kernels, attention_part(): pl.pallas_call(attention_kernel, out_shape=(jax.ShapeDtypeStruct((LPD, 10...  37.2 us
    unnamed x14, local copies, waits for them, and re-layouts  4.76 us

profile of v1, /device:TPU:1, one launch (start us, length us, event | category | flops | bytes accessed | tf_op | source)
XLA Modules:
  0.0 152.7 jit_solution(1415750598254739233)
XLA Ops:
  0.6 1.5 %reshape.114.lrows = s32[32,8,1]{2,1,0:T(8,128)} reshape(s32[256]{0:T(256)} %param.14) | data formatting | bytes 2048 | tf_op jit(solution)/shard_map/reshape | solution.py:636
  2.2 48.6 %gather.1 = (bf16[8,2,2,8,8192]{4,3,2,1,0:T(8,128)(2,1)}, bf16[8,2,2,320,128]{4,3,2,1,0:T(8,128)(2,1)}) custom-call(bf16[128,1024]{1,0:T(8,128)(2,1)} %hidden.1, bf16[128,1024]{1,0:T(8,128)(2,1)} %queries.1, bf16[128,128]{1,0:T(8,128)(2,1)} %keys.1, bf16[128,128]{1,0:T(8,128)(2,1)} %values.1, s32[32,8,1]{2,1,0:T(8,128)} %reshape.114.lrows), custom_call_target="tpu_custom_call" | custom-call | tf_op jit(solution)/shard_map/gather/pallas_call | solution.py:216
  50.8 0.0 copy-start.4
  50.8 0.0 copy-start.3
  50.8 56.3 %loss_part.1 = (f32[8,128]{1,0:T(8,128)}, bf16[256,256]{1,0:T(8,128)(2,1)}, bf16[8,32,256]{2,1,0:T(8,128)(2,1)}) custom-call(bf16[8,2,2,8,8192]{4,3,2,1,0:T(8,128)(2,1)} %get-tuple-element.13.rows, f32[1,8192]{1,0:T(1,128)} %bitcast.7, s32[1,256]{1,0:T(1,128)} %bitcast.8, bf16[594,8192]{1,0:T(8,128)(2,1)} %weight_hbm.1), custom_call_target="tpu_custom_call" | custom-call | tf_op jit(solution)/shard_map/loss_part/pallas_call | solution.py:434
  107.2 0.0 copy-start
  107.2 1.2 slice.9
  108.4 0.1 iota_add_fusion
  108.5 0.1 add.33.key_pos
  108.6 0.0 copy-start.1
  108.6 0.1 reshape.109
  108.7 0.1 reshape.110
  108.8 0.2 slice_reduce_fusion.1
  109.0 0.1 fusion.1
  109.1 0.1 reshape.111.query_pos
  109.2 0.0 copy-start.2
  109.2 0.7 copy.18.key_col
  110.0 0.1 dynamic-slice_bitcast_fusion
  110.1 0.7 copy.19.query_col
  110.8 37.2 %attention_part.1 = (bf16[8,1024]{1,0:T(8,128)(2,1)}, bf16[128,128]{1,0:T(8,128)(2,1)}, bf16[128,128]{1,0:T(8,128)(2,1)}) custom-call(bf16[8,32,256]{2,1,0:T(8,128)(2,1)} %get-tuple-element.15.resid, bf16[1024,256]{1,0:T(8,128)(2,1)} %out_weight.1, bf16[8,2,2,320,128]{4,3,2,1,0:T(8,128)(2,1)} %get-tuple-element.16.kvq, s32[1,4096]{1,0:T(1,128)} %copy-done.1, ...), custom_call_target="tpu_custom_call" | custom-call | tf_op jit(solution)/shard_map/attention_part/pallas_call | solution.py:583
  148.0 1.3 copy.24
  149.3 1.4 copy.25
  150.7 1.4 copy.26
  152.0 0.7 copy.27
  (8 shorter events, 0.0 us)
Async XLA Ops:
  50.8 57.6 %copy-start.4 = (s32[64]{0:T(128)S(1)}, s32[64]{0:T(128)}, u32[]{:S(2)}) copy-start(s32[64]{0:T(128)} %param.15) | copy-start | bytes 772
  50.8 57.8 %copy-start.3 = (s32[256]{0:T(256)S(1)}, s32[256]{0:T(256)}, u32[]{:S(2)}) copy-start(s32[256]{0:T(256)} %param.14) | copy-start | bytes 3076
  107.2 44.9 %copy-start = (bf16[256,256]{1,0:T(8,128)(2,1)S(1)}, bf16[256,256]{1,0:T(8,128)(2,1)}, u32[]{:S(2)}) copy-start(bf16[256,256]{1,0:T(8,128)(2,1)} %get-tuple-element.32) | copy-start | bytes 393220
  108.6 2.2 %copy-start.1 = (s32[1,4096]{1,0:T(1,128)}, s32[1,4096]{1,0:T(1,128)S(1)}, u32[]{:S(2)}) copy-start(s32[1,4096]{1,0:T(1,128)S(1)} %add.33.key_pos) | copy-start | bytes 49156
  109.2 1.6 %copy-start.2 = (s32[1,2048]{1,0:T(1,128)}, s32[1,2048]{1,0:T(1,128)S(1)}, u32[]{:S(2)}) copy-start(s32[1,2048]{1,0:T(1,128)S(1)} %reshape.111.query_pos) | copy-start | bytes 24580

commit v2 on v1

v2 whole, which is shorter than its diff:
```python
import functools

import jax
import jax.numpy as jnp
from jax import lax
from jax.experimental import pallas as pl
from jax.experimental.pallas import tpu as pltpu
from jax.sharding import PartitionSpec as P

MESH = pl.DeviceIdType.MESH
F32 = jnp.float32
BF16 = jnp.bfloat16

HEAD = 128
ROWS = 256
WIDTH = 8192
NV, NC, NZ = 8, 32, 8
LPD = 8
VOC = 594
PAD = 640
KVQ = 320
EPS = 1e-06
GRAD_WEIGHT = 16.0
SCALE = HEAD ** (-0.5)
FILL = -1e30

ORDERS = (
    (("x", 1), ("x", 3), ("y", 1), ("y", 3)),
    (("x", 3), ("x", 1), ("y", 3), ("y", 1)),
    (("y", 1), ("y", 3), ("x", 1), ("x", 3)),
    (("y", 3), ("y", 1), ("x", 3), ("x", 1)),
)


class Place:
    def __init__(self):
        self.v = lax.axis_index("vocab")
        self.c = lax.axis_index("ctx")
        self.xl = lax.div(self.v, 4)
        self.y = lax.rem(self.v, 4)
        self.z = lax.div(self.c, 4)
        self.xh = lax.rem(lax.div(self.c, 2), 2)
        self.core = lax.rem(self.c, 2)

    def y_off(self, off):
        y = self.y
        if off == 0:
            return y
        if off == 1:
            return y + 1 - 2 * lax.rem(y, 2)
        if off == 2:
            return lax.rem(y + 2, 4)
        return 3 - y

    def xl_off(self, off):
        return 1 - self.xl if off & 1 else self.xl

    def xh_off(self, off):
        return 1 - self.xh if off & 2 else self.xh

    def v_at(self, x_off=0, y_off=0):
        return self.xl_off(x_off) * 4 + self.y_off(y_off)

    def dev(self, x_off=0, y_off=0, z=None, core_off=0):
        z = self.z if z is None else z
        core = 1 - self.core if core_off else self.core
        return (self.v_at(x_off, y_off), z * 4 + self.xh_off(x_off) * 2 + core)

    def z_plus(self, d):
        return lax.rem(self.z + d + NZ, NZ)


def greet(devices):
    barrier = pltpu.get_barrier_semaphore()
    for device in devices:
        pl.semaphore_signal(barrier, inc=1, device_id=device, device_id_type=MESH)
    return functools.partial(pl.semaphore_wait, barrier, len(devices))


def remote(src, dst, send, recv, device):
    copy = pltpu.make_async_remote_copy(
        src_ref=src, dst_ref=dst, send_sem=send, recv_sem=recv, device_id=device, device_id_type=MESH
    )
    copy.start()
    return copy


def offsets(order, done):
    held = [(0, 0)]
    for axis, mask in order[:done]:
        held = held + [(ox ^ mask, oy) if axis == "x" else (ox, oy ^ mask) for ox, oy in held]
    return held


def partner(me, axis, mask):
    return me.dev(x_off=mask) if axis == "x" else me.dev(y_off=mask)


def column(row_vector, width=128):
    return jnp.transpose(jnp.broadcast_to(row_vector, (width, row_vector.shape[1])))


def merge(parts):
    top = jnp.max(parts[:, 0:2], axis=0)
    weight = jnp.exp(parts[:, 0:2] - top[None])
    total = jnp.sum(parts[:, 2:4] * weight, axis=0)
    first = jnp.sum(parts[:, 4:6] * weight, axis=0)
    hit = jnp.sum(parts[:, 6:8], axis=0)
    return jnp.concatenate([top, total, first, hit], axis=0)


def wide(two):
    return jnp.concatenate([two[0:1], two[1:2]], axis=1)


def step_kernel(
    hidden, queries, keys, values, lrows, targets, gain, key_pos, query_pos, out_weight, weight_hbm,
    loss, resid_t, dq, dk, dv,
    weight, rows, y, kvq, logits, grad_t, rms_col, inner_col, st1, st2, cs, cr, acc,
    sb1, sb2, sb3, sb4, rb1, rb2, rb3, rb4, zs, zr, resid,
    k_all, v_all, q_all, probs, part, pc, pr, rs, rr, grads, extras, square_tile, s2,
    w_sem, z_s, z_r, a_s, a_r, f_s, f_r, k_s, k_r, kf_s, kf_r, s1_s, s1_r, s2_s, s2_r,
    c_s, c_r, x_s, x_r, t_s, t_r, v_s, v_r, pc_s, pc_r, r_s, r_r, g_s, g_r, e_s, e_r, fg_s, fg_r, fe_s, fe_r,
):
    me = Place()
    mate = me.dev(core_off=1)
    group1 = [(d, o) for d in range(NZ) for o in range(2) if (d, o) != (0, 0)]
    group2 = [(ox, oy) for ox in range(4) for oy in range(4) if (ox, oy) != (0, 0)]
    peers = [(d, o) for d in range(NZ) for o in (0, 2) if (d, o) != (0, 0)]
    greeted = greet(
        [me.dev(z=me.z_plus(d), core_off=o) for d, o in group1]
        + [me.dev(ox, oy) for ox, oy in group2]
        + [me.dev(z=me.z_plus(d), x_off=2) for d in range(1, NZ)]
    )
    loads = []
    for j in range(8):
        section = (slice(None), slice(1024 * j, 1024 * j + 1024))
        load = pltpu.make_async_copy(weight_hbm.at[section], weight.at[section], w_sem.at[j])
        load.start()
        loads.append(load)
    started = []

    def go(*args):
        copy = remote(*args)
        started.append(copy)
        return copy

    lane = lax.broadcasted_iota(jnp.int32, (LPD, ROWS), 1)
    line = lax.broadcasted_iota(jnp.int32, (LPD, ROWS), 0)
    own = jnp.sum(jnp.where(lane == me.c * LPD + line, lrows[...], 0.0), axis=1, keepdims=True)
    rows_at = lax.broadcasted_iota(jnp.int32, (LPD, 128), 1).astype(F32)
    pick = (own == rows_at).astype(F32).astype(BF16)
    mine_cols = pl.ds(pl.multiple_of(me.v * 1024, 1024), 1024)
    rows[me.z, me.xh, me.core, :, mine_cols] = jnp.dot(
        pick, hidden[...], preferred_element_type=F32
    ).astype(BF16)
    picked_q = jnp.dot(pick, queries[...], preferred_element_type=F32).astype(BF16)
    kvq[me.z, me.xh, me.core, 0:128, :] = keys[...]
    kvq[me.z, me.xh, me.core, 128:256, :] = values[...]
    for head in range(8):
        kvq[me.z, me.xh, me.core, 256 + 8 * head : 264 + 8 * head, :] = picked_q[:, 128 * head : 128 * head + 128]
    greeted()

    def block(k, off):
        cols = pl.ds(pl.multiple_of(me.v_at(*off) * 1024, 1024), 1024)
        return rows.at[pl.ds(2 * k, 2), me.xh_off(off[0]), me.core, :, cols]

    own_block = rows.at[me.z, me.xh, me.core, :, mine_cols]
    z_copies = [
        go(own_block, own_block, z_s.at[d], z_r.at[d], me.dev(z=me.z_plus(d))) for d in range(1, NZ)
    ]
    own_kvq = kvq.at[me.z, me.xh, me.core]
    k_x = go(own_kvq, own_kvq, k_s.at[0], k_r.at[0], me.dev(x_off=2))
    for copy in z_copies:
        copy.wait_recv()

    a_copies, f_copies, kf_copies, ring = {}, [], [], {}

    def spread(k, index, off, first):
        here = block(k, off)
        for step in range(first, 4):
            slot = (1 << step) - 1 + index
            a_copies[k, step, index] = go(
                here, here, a_s.at[k, slot], a_r.at[k, slot], partner(me, *ORDERS[k][step])
            )
        f_copies.append(go(here, here, f_s.at[k, index], f_r.at[k, index], mate))

    def arrive(step, js):
        for j in js:
            for k, order in enumerate(ORDERS):
                a_copies[k, step, j].wait_recv()
                index = (1 << step) + j
                spread(k, index, offsets(order, step + 1)[index], step + 1)

    def ring_step(step):
        lo, hi = (0, KVQ) if step < 4 else (0, 160)
        lo2, hi2 = (0, KVQ) if step < 4 else (160, KVQ)
        up, down = me.z_plus(-(step - 1)), me.z_plus(step - 1)
        right = kvq.at[up, :, me.core, lo:hi]
        left = kvq.at[down, :, me.core, lo2:hi2]
        ring[step] = (
            go(right, right, k_s.at[2 * step - 1], k_r.at[2 * step - 1], me.dev(z=me.z_plus(1))),
            go(left, left, k_s.at[2 * step], k_r.at[2 * step], me.dev(z=me.z_plus(-1))),
        )

    def ring_forward(slot, z):
        here = kvq.at[z, :, me.core]
        kf_copies.append(go(here, here, kf_s.at[slot], kf_r.at[slot], mate))

    def ring_wait(step):
        ring[step][0].wait_recv()
        if step < 4:
            ring_forward(2 * step - 1, me.z_plus(-step))
        ring[step][1].wait_recv()
        ring_forward(2 * step if step < 4 else 7, me.z_plus(step))

    for k in range(4):
        spread(k, 0, (0, 0), 0)
    arrive(0, range(1))
    k_x.wait_recv()
    ring_step(1)
    ring_forward(0, me.z)
    arrive(1, range(2))
    arrive(2, range(4))
    ring_wait(1)
    ring_step(2)
    arrive(3, range(4))
    ring_wait(2)
    ring_step(3)
    arrive(3, range(4, 8))
    for copy in f_copies:
        copy.wait_recv()

    def prepare(j, square):
        cols = pl.ds(pl.multiple_of(j * 1024, 1024), 1024)
        x = rows[:, :, :, :, cols].astype(F32).reshape(ROWS, 1024)
        y[:, cols] = (x * gain[:, cols]).astype(BF16)
        sq = x * x
        for t in range(8):
            square = square + sq[:, 128 * t : 128 * t + 128]
        return square

    square = lax.fori_loop(0, 8, prepare, jnp.zeros((ROWS, 128), F32))
    inv_col = lax.rsqrt(jnp.sum(square, axis=1, keepdims=True) * (1.0 / WIDTH) + EPS)
    rms_col[...] = jnp.broadcast_to(inv_col, (ROWS, 128))
    inv_row = jnp.transpose(rms_col[...])[0:1, :]

    logits[PAD - 48 : PAD, :] = jnp.zeros((48, ROWS), F32)
    for j in range(8):
        loads[j].wait()
        term = lax.dot_general(
            weight[:, 1024 * j : 1024 * j + 1024], y[:, 1024 * j : 1024 * j + 1024],
            (((1,), (1,)), ((), ())), preferred_element_type=F32,
        )
        logits[0:VOC, :] = term if j == 0 else logits[0:VOC, :] + term
        if j == 3:
            ring_wait(3)
            ring_step(4)

    ids = lax.broadcasted_iota(jnp.int32, (PAD, ROWS), 0)
    real = ids < VOC
    first_id = (me.v * NC + me.c) * VOC
    is_target = ((ids + first_id) == targets[...]) & real
    value = jnp.where(real, logits[...] * inv_row, FILL)
    logits[...] = value
    top = jnp.max(value, axis=0, keepdims=True)
    raw = jnp.exp(value - top)
    stats = (
        top,
        jnp.sum(raw, axis=0, keepdims=True),
        jnp.sum(raw * value, axis=0, keepdims=True),
        jnp.sum(jnp.where(is_target, value, 0.0), axis=0, keepdims=True),
    )
    packed = jnp.concatenate([piece[:, h : h + 128] for piece in stats for h in (0, 128)], axis=0)
    slot1 = me.z * 2 + me.core
    st1[slot1] = packed
    waits = []
    for i, (d, o) in enumerate(group1):
        waits.append(
            go(st1.at[slot1], st1.at[slot1], s1_s.at[i], s1_r.at[2 * d + o], me.dev(z=me.z_plus(d), core_off=o))
        )
    ring_wait(4)
    for copy in kf_copies:
        copy.wait_recv()

    k_all[...] = kvq[:, :, :, 0:128, :].reshape(NC * 128, HEAD)
    v_all[...] = kvq[:, :, :, 128:256, :].reshape(NC * 128, HEAD)
    q_all[...] = kvq[:, :, :, 256:320, :].reshape(NC * 64, HEAD)
    q_own = kvq[me.z, me.xh, me.core, 256:320, :]
    lane = lax.broadcasted_iota(jnp.int32, (64, NC * 64), 1)
    line = lax.broadcasted_iota(jnp.int32, (64, NC * 64), 0)
    query_col = jnp.sum(jnp.where(lane == me.c * 64 + line, query_pos[...], 0.0), axis=1, keepdims=True)
    for copy in waits:
        copy.wait_recv()
    slot2 = (me.xh * 2 + me.xl) * 4 + me.y
    st2[slot2] = merge(st1[...])
    waits = []
    for i, (ox, oy) in enumerate(group2):
        waits.append(go(st2.at[slot2], st2.at[slot2], s2_s.at[i], s2_r.at[4 * ox + oy], me.dev(ox, oy)))
    scores = lax.dot_general(q_own, k_all[...], (((1,), (1,)), ((), ())), preferred_element_type=F32)
    seen = key_pos[...] <= query_col
    masked = jnp.where(seen, scores * SCALE, FILL)
    top = jnp.max(masked, axis=1, keepdims=True)
    raw = jnp.where(seen, jnp.exp(masked - top), 0.0)
    total = jnp.sum(raw, axis=1, keepdims=True)
    probs[...] = raw / total
    row_log_total = top + jnp.log(total)

    for copy in waits:
        copy.wait_recv()
    final = merge(st2[...])
    log_total = wide(final[0:2] + jnp.log(final[2:4]))
    hit = wide(final[6:8])
    grad = GRAD_WEIGHT * (jnp.exp(logits[...] - log_total) - is_target.astype(F32))
    grad_t[...] = jnp.transpose(grad).astype(BF16)

    def chunk(z, xh, core):
        cols = pl.ds(pl.multiple_of((z * 4 + xh * 2 + core) * 256, 256), 256)
        return jnp.dot(grad_t[:, 0:VOC], weight[:, cols], preferred_element_type=F32).reshape(NV, 32, 256)

    c_copies = {}
    z_order = (0, 2, 4, 6, 1, 3, 5, 7)
    for z in z_order:

        def other(xh, _, z=z):
            cs[z, xh] = chunk(z, xh, 1 - me.core).astype(BF16)
            return 0

        lax.fori_loop(0, 2, other, 0)
        c_copies[z] = go(cs.at[z], cr.at[z], c_s.at[z], c_r.at[z], mate)

    sends, recvs = (sb1, sb2, sb3, sb4), (rb1, rb2, rb3, rb4)
    moving = {}

    def at(z, off):
        return (z, me.xh_off(off[0]), me.v_at(*off))

    def halve(z, step):
        back = ORDERS[z // 2]
        axis, mask = back[3 - step]
        keep, before = offsets(back, 3 - step), offsets(back, 4 - step)
        for off in before:
            here = at(z, off)
            if step == 0:
                extra = cr[here].astype(F32)
            else:
                extra = recvs[step - 1][z, before.index(off)].astype(F32)
            summed = acc[here] + extra
            away = (off[0] ^ mask, off[1]) if axis == "x" else (off[0], off[1] ^ mask)
            if away in keep:
                sends[step][z, keep.index(away)] = summed.astype(BF16)
            else:
                acc[here] = summed
        moving[z, step] = go(
            sends[step].at[z], recvs[step].at[z], x_s.at[z, step], x_r.at[z, step], partner(me, axis, mask)
        )

    for z in z_order:

        def mine(xh, _, z=z):
            acc[z, xh] = chunk(z, xh, me.core)
            return 0

        lax.fori_loop(0, 2, mine, 0)
        c_copies[z].wait_recv()
        halve(z, 0)
    for step in range(1, 4):
        for z in z_order:
            moving[z, step - 1].wait_recv()
            halve(z, step)

    def z_copy(z, src):
        return pltpu.make_async_remote_copy(
            src_ref=zs.at[z], dst_ref=zr.at[src], send_sem=t_s.at[z], recv_sem=t_r.at[src],
            device_id=me.dev(z=jnp.int32(z)), device_id_type=MESH,
        )

    for z in z_order:
        moving[z, 3].wait_recv()
        zs[z] = (acc[at(z, (0, 0))] + rb4[z, 0].astype(F32)).astype(BF16)

        @pl.when(me.z != z)
        def _(z=z):
            z_copy(z, me.z).start()

    loss[...] = jnp.broadcast_to(jnp.mean(log_total - hit, axis=1, keepdims=True), (8, 128))
    inner_col[...] = column((wide(final[4:6] / final[2:4]) - hit) * (GRAD_WEIGHT / WIDTH))
    k_own = kvq[me.z, me.xh, me.core, 0:128, :]
    v_own = kvq[me.z, me.xh, me.core, 128:256, :]
    s2[...] = lax.dot_general(k_own, q_all[...], (((1,), (1,)), ((), ())), preferred_element_type=F32)
    zr[me.z] = zs[me.z]
    for z in range(NZ):

        @pl.when(me.z != z)
        def _(z=z):
            z_copy(z, z).wait_recv()

    normed_grad = jnp.sum(zr[...].astype(F32), axis=0)
    cols = pl.ds(pl.multiple_of(me.c * 256, 256), 256)
    lines = pl.ds(pl.multiple_of(me.v * 32, 32), 32)
    inv = rms_col[lines, 0:1]
    picked = rows[me.v, :, :, :, cols].astype(F32).reshape(32, 256)
    out = inv * (normed_grad * gain[:, cols] - picked * (inv * inner_col[lines, 0:1]))
    resid[me.v] = out.astype(BF16)
    v_copies = []
    for i, (ox, oy) in enumerate([(o, q) for o in range(2) for q in range(4) if (o, q) != (0, 0)]):
        v_copies.append(go(resid.at[me.v], resid.at[me.v], v_s.at[i], v_r.at[i], me.dev(ox, oy)))
    high = probs[...].astype(BF16)
    low = (probs[...] - high.astype(F32)).astype(BF16)
    attn_out = jnp.dot(high, v_all[...], preferred_element_type=F32) + jnp.dot(
        low, v_all[...], preferred_element_type=F32
    )
    for copy in v_copies:
        copy.wait_recv()

    wide_part = lax.dot_general(
        resid[...].reshape(ROWS, 256), out_weight[...], (((1,), (1,)), ((), ())), preferred_element_type=F32
    )
    for h in range(8):
        part[:, :, :, 8 * h : 8 * h + 8, :] = wide_part[:, 128 * h : 128 * h + 128].reshape(NZ, 2, 2, LPD, HEAD)
    pc[...] = part[:, :, 1 - me.core].astype(BF16)
    pc_copy = go(pc, pr, pc_s, pc_r, mate)
    resid_t[...] = jnp.transpose(resid[...].astype(F32).reshape(ROWS, 256)).astype(BF16)
    pc_copy.wait_recv()
    rs[...] = (part[:, :, me.core] + pr[...].astype(F32)).astype(BF16)
    r_copies = []
    for i, (d, o) in enumerate(peers):
        z, xh = me.z_plus(d), me.xh_off(o)
        r_copies.append(go(rs.at[z, xh], rr.at[me.z, me.xh], r_s.at[i], r_r.at[i], me.dev(z=z, x_off=o)))
    rr[me.z, me.xh] = rs[me.z, me.xh]
    for copy in r_copies:
        copy.wait_recv()
    grad_own = jnp.sum(rr[...].astype(F32), axis=(0, 1)).astype(BF16)
    grads[me.z, me.xh, me.core] = grad_own
    delta = jnp.sum(grad_own.astype(F32) * attn_out, axis=1, keepdims=True)
    lane = lax.broadcasted_iota(jnp.int32, (64, 128), 1)
    square_tile[...] = jnp.zeros((128, 128), F32)
    square_tile[0:64, :] = jnp.where(lane == 0, delta, jnp.where(lane == 1, row_log_total, 0.0))
    extras[me.z, me.xh, me.core] = jnp.transpose(square_tile[...])[0:8, :]
    own_g, own_e = grads.at[me.z, me.xh, me.core], extras.at[me.z, me.xh, me.core]
    g_copies = []
    for i, (d, o) in enumerate(peers):
        device = me.dev(z=me.z_plus(d), x_off=o)
        g_copies.append(
            (
                go(own_g, own_g, g_s.at[i], g_r.at[i], device),
                go(own_e, own_e, e_s.at[i], e_r.at[i], device),
                d,
                o,
            )
        )
    forwards = [
        go(own_g, own_g, fg_s.at[15], fg_r.at[15], mate),
        go(own_e, own_e, fe_s.at[15], fe_r.at[15], mate),
    ]
    prob_grad = lax.dot_general(grad_own, v_all[...], (((1,), (1,)), ((), ())), preferred_element_type=F32)
    score_grad = (probs[...] * (prob_grad - delta)).astype(BF16)
    query_grad = jnp.dot(score_grad, k_all[...], preferred_element_type=F32) * SCALE
    for h in range(8):
        dq[:, 128 * h : 128 * h + 128] = query_grad[8 * h : 8 * h + 8, :].astype(BF16)
    for i, (g_copy, e_copy, d, o) in enumerate(g_copies):
        z, xh = me.z_plus(-d), me.xh_off(o)
        g_copy.wait_recv()
        e_copy.wait_recv()
        here_g, here_e = grads.at[z, xh, me.core], extras.at[z, xh, me.core]
        forwards.append(go(here_g, here_g, fg_s.at[i], fg_r.at[i], mate))
        forwards.append(go(here_e, here_e, fe_s.at[i], fe_r.at[i], mate))
    own_key_pos = key_pos[:, pl.ds(pl.multiple_of(me.c * 128, 128), 128)]
    lane = lax.broadcasted_iota(jnp.int32, (128, 128), 1)
    line = lax.broadcasted_iota(jnp.int32, (128, 128), 0)
    key_col = jnp.sum(jnp.where(lane == line, own_key_pos, 0.0), axis=1, keepdims=True)
    seen2 = key_col <= query_pos[...]
    for copy in forwards:
        copy.wait_recv()
    grads_all = grads[...].reshape(NC * 64, HEAD)
    e_all = extras[...].reshape(NC, 8, 128)
    delta_all = jnp.concatenate([e_all[i, 0:1, 0:64] for i in range(NC)], axis=1)
    log_all = jnp.concatenate([e_all[i, 1:2, 0:64] for i in range(NC)], axis=1)
    probs2 = jnp.where(seen2, jnp.exp(s2[...] * SCALE - log_all), 0.0)
    dv[...] = jnp.dot(probs2.astype(BF16), grads_all, preferred_element_type=F32).astype(BF16)
    prob_grad2 = lax.dot_general(v_own, grads_all, (((1,), (1,)), ((), ())), preferred_element_type=F32)
    score_grad2 = (probs2 * (prob_grad2 - delta_all)).astype(BF16)
    dk[...] = (jnp.dot(score_grad2, q_all[...], preferred_element_type=F32) * SCALE).astype(BF16)
    for copy in started:
        copy.wait_send()
    for z in range(NZ):

        @pl.when(me.z != z)
        def _(z=z):
            z_copy(z, me.z).wait_send()


def step(*operands):
    vmem = pl.BlockSpec(memory_space=pltpu.VMEM)
    dma = pltpu.SemaphoreType.DMA
    scratch = pltpu.VMEM
    halves = [8, 4, 2, 1]
    return pl.pallas_call(
        step_kernel,
        out_shape=(
            jax.ShapeDtypeStruct((8, 128), F32),
            jax.ShapeDtypeStruct((256, ROWS), BF16),
            jax.ShapeDtypeStruct((LPD, 1024), BF16),
            jax.ShapeDtypeStruct((128, HEAD), BF16),
            jax.ShapeDtypeStruct((128, HEAD), BF16),
        ),
        in_specs=[vmem] * 10 + [pl.BlockSpec(memory_space=pl.ANY)],
        out_specs=(vmem,) * 5,
        scratch_shapes=[
            scratch((VOC, WIDTH), BF16),
            scratch((NZ, 2, 2, LPD, WIDTH), BF16),
            scratch((ROWS, WIDTH), BF16),
            scratch((NZ, 2, 2, KVQ, HEAD), BF16),
            scratch((PAD, ROWS), F32),
            scratch((ROWS, PAD), BF16),
            scratch((ROWS, 128), F32),
            scratch((ROWS, 128), F32),
            scratch((16, 8, 128), F32),
            scratch((16, 8, 128), F32),
            scratch((NZ, 2, NV, 32, 256), BF16),
            scratch((NZ, 2, NV, 32, 256), BF16),
            scratch((NZ, 2, NV, 32, 256), F32),
            *[scratch((NZ, n, 32, 256), BF16) for n in halves],
            *[scratch((NZ, n, 32, 256), BF16) for n in halves],
            scratch((NZ, 32, 256), BF16),
            scratch((NZ, 32, 256), BF16),
            scratch((NV, 32, 256), BF16),
            scratch((NC * 128, HEAD), BF16),
            scratch((NC * 128, HEAD), BF16),
            scratch((NC * 64, HEAD), BF16),
            scratch((64, NC * 128), F32),
            scratch((NZ, 2, 2, 64, HEAD), F32),
            *[scratch((NZ, 2, 64, HEAD), BF16)] * 4,
            scratch((NZ, 2, 2, 64, HEAD), BF16),
            scratch((NZ, 2, 2, 8, 128), F32),
            scratch((128, 128), F32),
            scratch((128, NC * 64), F32),
            dma((8,)), dma((NZ,)), dma((NZ,)), dma((4, 15)), dma((4, 15)), dma((4, 16)), dma((4, 16)),
            dma((9,)), dma((9,)), dma((8,)), dma((8,)),
            dma((16,)), dma((16,)), dma((16,)), dma((16,)), dma((NZ,)), dma((NZ,)),
            dma((NZ, 4)), dma((NZ, 4)), dma((NZ,)), dma((NZ,)), dma((7,)), dma((7,)),
            dma, dma, dma((15,)), dma((15,)), dma((15,)), dma((15,)), dma((15,)), dma((15,)),
            dma((16,)), dma((16,)), dma((16,)), dma((16,)),
        ],
        compiler_params=pltpu.CompilerParams(
            collective_id=0, has_side_effects=True, vmem_limit_bytes=61 * 1024 * 1024
        ),
        name="step",
    )(*operands)


def emit_kernel(loss, resid_t, dq, dk, dv, loss_out, resid_out, dq_out, dk_out, dv_out):
    loss_out[0, 0] = loss[0, 0]
    resid_out[...] = resid_t[...]
    dq_out[...] = dq[...]
    dk_out[...] = dk[...]
    dv_out[...] = dv[...]


def emit(loss, *results):
    vmem = pl.BlockSpec(memory_space=pltpu.VMEM)
    return pl.pallas_call(
        emit_kernel,
        out_shape=(jax.ShapeDtypeStruct((1, 1), F32),)
        + tuple(jax.ShapeDtypeStruct(array.shape, array.dtype) for array in results),
        in_specs=[vmem] * 5,
        out_specs=(pl.BlockSpec(memory_space=pltpu.SMEM),) + (vmem,) * 4,
        name="emit",
    )(loss, *results)


def per_device(
    hidden,
    norm_gain,
    head_weight,
    targets,
    loss_rows,
    stretch_of_slot,
    queries,
    key_states,
    attention_values,
    output_weight,
):
    spans = stretch_of_slot.reshape(NC, 2)
    local = loss_rows.reshape(NC, LPD)
    place = jnp.where(local < 64, spans[:, 0:1], spans[:, 1:2]) * 64 + lax.rem(local, 64)
    query_pos = jnp.broadcast_to(place[:, None, :], (NC, 8, LPD)).reshape(1, NC * 64).astype(F32)
    key_pos = stretch_of_slot[:, None] * 64 + lax.broadcasted_iota(jnp.int32, (64, 64), 1)
    key_pos = key_pos.reshape(1, 4096).astype(F32)
    loss, resid_t, dq, dk, dv = step(
        hidden,
        queries,
        key_states,
        attention_values,
        loss_rows.astype(F32).reshape(1, ROWS),
        targets.reshape(1, ROWS),
        norm_gain.reshape(1, WIDTH),
        key_pos,
        query_pos,
        output_weight,
        head_weight,
    )
    loss, resid_t, dq, dk, dv = emit(loss, resid_t, dq, dk, dv)
    return (loss[0, 0], dq, dk, dv, resid_t)


def solution(mesh):
    placed = (
        P("ctx", "vocab"),
        P(),
        P(("vocab", "ctx"), None),
        P(),
        P(),
        P(),
        P("ctx", "vocab"),
        P("ctx", "vocab"),
        P("ctx", "vocab"),
        P("vocab", "ctx"),
    )
    return jax.shard_map(
        per_device,
        mesh=mesh,
        in_specs=placed,
        out_specs=(P(), P("ctx", "vocab"), P("ctx", "vocab"), P("ctx", "vocab"), P("ctx", None)),
        check_vma=False,
    )
```

time: 153 us -> 127 us (0.83)
  Pallas kernels: 142 us -> 121 us
  local copies, waits for them, and re-layouts: 9.65 us -> 3.12 us
  other arithmetic: 0.15 us -> 2.06 us
    pallas_call x3 -> x2, Pallas kernels: 142 us -> 121 us  [the longest x1 119 us: step(): pl.pallas_call(step_kernel, out_shape=(jax.ShapeDtypeStruct((8, 128), F32...]
    unnamed x14 -> x0, local copies, waits for them, and re-layouts: 4.76 us -> none
    reshape x6 -> x0, local copies, waits for them, and re-layouts: 3.19 us -> none  [the longest x1 1.54 us: per_device(): loss_rows.reshape(NC, LPD, 1)]
where the time goes in v2:
time: 127 us
  Pallas kernels  121 us (95%)
  local copies, waits for them, and re-layouts  3.12 us (2%)
  other arithmetic  2.06 us (2%)
    pallas_call x1, Pallas kernels, step(): pl.pallas_call(step_kernel, out_shape=(jax.ShapeDtypeStruct((8, 128), F32...  119 us

profile of v2, /device:TPU:1, one launch (start us, length us, event | category | flops | bytes accessed | tf_op | source)
XLA Modules:
  0.0 126.9 jit_solution(5105892645829790086)
XLA Ops:
  0.6 0.7 broadcast_multiply_fusion
  1.3 1.2 convert_element_type.13
  2.5 0.8 reshape.118
  3.3 0.8 reshape.119
  4.1 0.2 slice_reduce_fusion.1
  4.2 0.1 fusion.2
  4.3 0.1 add_convert_fusion
  4.4 0.7 convert_element_type.15.key_pos
  5.1 0.7 convert_element_type.17.query_pos
  5.8 119.3 %step.1 = (f32[8,128]{1,0:T(8,128)}, bf16[256,256]{1,0:T(8,128)(2,1)}, bf16[8,1024]{1,0:T(8,128)(2,1)}, bf16[128,128]{1,0:T(8,128)(2,1)}, bf16[128,128]{1,0:T(8,128)(2,1)}) custom-call(bf16[128,1024]{1,0:T(8,128)(2,1)} %hidden.1, bf16[128,1024]{1,0:T(8,128)(2,1)} %queries.1, bf16[128,128]{1,0:T(8,128)(2,1)} %keys.1, bf16[128,128]{1,0:T(8,128)(2,1)} %values.1, ...), custom_call_target="tpu_custom_call" | custom-call | tf_op jit(solution)/shard_map/step/pallas_call | solution.py:498
  125.1 1.6 %emit.1 = (f32[1,1]{1,0:T(1,128)}, bf16[256,256]{1,0:T(8,128)(2,1)}, bf16[8,1024]{1,0:T(8,128)(2,1)}, bf16[128,128]{1,0:T(8,128)(2,1)}, bf16[128,128]{1,0:T(8,128)(2,1)}) custom-call(f32[8,128]{1,0:T(8,128)} %get-tuple-element.15.loss, bf16[256,256]{1,0:T(8,128)(2,1)} %get-tuple-element.16.resid_t, bf16[8,1024]{1,0:T(8,128)(2,1)} %get-tuple-element.17.dq, ...), custom_call_target="tpu_custom_call" | custom-call | tf_op jit(solution)/shard_map/emit/pallas_call | solution.py:562
  (1 shorter events, 0.0 us)

commit v3 on v2

--- a/solution.py
+++ b/solution.py
@@ -31,6 +31,15 @@
     (("y", 3), ("y", 1), ("x", 3), ("x", 1)),
 )
 
+NEAR_FIRST = (0, 1, 7, 2, 6, 3, 5, 4)
+FAR_FIRST = (4, 3, 5, 2, 6, 1, 7, 0)
+COLOUR = {d: i % 4 for i, d in enumerate(NEAR_FIRST)}
+
+GATHER = (
+    ("z", 0), ("z", 3), ("z", 1), (0, 0), ("z", 2), ("r", 1), (3, 0), (1, 0), (0, 1), (2, 0), (3, 1), (1, 1), (0, 2),
+    (2, 1), (3, 2), (1, 2), ("r", 2), (0, 3), (2, 2), (3, 3), ("p", 0), (1, 3), ("p", 3), (2, 3), ("p", 1), ("p", 2),
+)
+
 
 class Place:
     def __init__(self):
@@ -92,6 +101,29 @@
     return held
 
 
+def pieces(me, order, step):
+    every = slice(None)
+    if step < 0:
+        return [(me.xh, me.xl, me.y)]
+    axis, mask = order[step]
+    second = step in (1, 3)
+    first_mask = order[step - 1][1] if second else 0
+    other = step >= 2
+    if axis == "x":
+        y = every if other else me.y
+        if not second:
+            return [(me.xh_off(mask), me.xl_off(mask), y)]
+        if first_mask == 1:
+            return [(me.xh_off(mask), every, y)]
+        return [(me.xh_off(m), me.xl_off(m), y) for m in (mask, mask ^ first_mask)]
+    xh, xl = (every, every) if other else (me.xh, me.xl)
+    if not second:
+        return [(xh, xl, me.y_off(mask))]
+    if first_mask == 1:
+        return [(xh, xl, pl.ds(2 - 2 * lax.div(me.y, 2), 2))]
+    return [(xh, xl, me.y_off(m)) for m in (mask, mask ^ first_mask)]
+
+
 def partner(me, axis, mask):
     return me.dev(x_off=mask) if axis == "x" else me.dev(y_off=mask)
 
@@ -114,23 +146,30 @@
 
 
 def step_kernel(
-    hidden, queries, keys, values, lrows, targets, gain, key_pos, query_pos, out_weight, weight_hbm,
+    hidden_hbm, queries_hbm, keys_hbm, values_hbm, lrows_hbm, targets_hbm, gain_hbm, stretch_hbm, out_hbm, weight_hbm,
     loss, resid_t, dq, dk, dv,
     weight, rows, y, kvq, logits, grad_t, rms_col, inner_col, st1, st2, cs, cr, acc,
     sb1, sb2, sb3, sb4, rb1, rb2, rb3, rb4, zs, zr, resid,
-    k_all, v_all, q_all, probs, part, pc, pr, rs, rr, grads, extras, square_tile, s2,
-    w_sem, z_s, z_r, a_s, a_r, f_s, f_r, k_s, k_r, kf_s, kf_r, s1_s, s1_r, s2_s, s2_r,
-    c_s, c_r, x_s, x_r, t_s, t_r, v_s, v_r, pc_s, pc_r, r_s, r_r, g_s, g_r, e_s, e_r, fg_s, fg_r, fe_s, fe_r,
+    k_all, v_all, q_all, probs, part, pc, pr, rs, rx, rz, rr, grads, extras, square_tile, s2,
+    key_pos, query_pos, gain, out_weight, hidden, queries, lrows_in, targets_in, gain_in, stretch, w_sem, o_sem, i_sem, z_s, z_r, a_s, a_r, f_s, f_r, k_s, k_r, kf_s, kf_r, s1_s, s1_r, s2_s, s2_r,
+    c_s, c_r, x_s, x_r, t_s, t_r, v_s, v_r, pc_s, pc_r, rx_s, rx_r, r_s, r_r, g_s, g_r, e_s, e_r, gx_s, gx_r, fg_s, fg_r, ex_s, ex_r, fe_s, fe_r,
 ):
     me = Place()
     mate = me.dev(core_off=1)
     group1 = [(d, o) for d in range(NZ) for o in range(2) if (d, o) != (0, 0)]
     group2 = [(ox, oy) for ox in range(4) for oy in range(4) if (ox, oy) != (0, 0)]
-    peers = [(d, o) for d in range(NZ) for o in (0, 2) if (d, o) != (0, 0)]
+    arrivals = []
+    for i, (src, dst) in enumerate([
+        (lrows_hbm, lrows_in), (hidden_hbm, hidden), (queries_hbm, queries),
+        (keys_hbm, kvq.at[me.z, me.xh, me.core, 0:128]), (values_hbm, kvq.at[me.z, me.xh, me.core, 128:256]),
+        (targets_hbm, targets_in), (gain_hbm, gain_in), (stretch_hbm, stretch),
+    ]):
+        arrival = pltpu.make_async_copy(src, dst, i_sem.at[i])
+        arrival.start()
+        arrivals.append(arrival)
     greeted = greet(
         [me.dev(z=me.z_plus(d), core_off=o) for d, o in group1]
         + [me.dev(ox, oy) for ox, oy in group2]
-        + [me.dev(z=me.z_plus(d), x_off=2) for d in range(1, NZ)]
     )
     loads = []
     for j in range(8):
@@ -138,6 +177,8 @@
         load = pltpu.make_async_copy(weight_hbm.at[section], weight.at[section], w_sem.at[j])
         load.start()
         loads.append(load)
+    out_load = pltpu.make_async_copy(out_hbm, out_weight, o_sem)
+    out_load.start()
     started = []
 
     def go(*args):
@@ -145,52 +186,71 @@
         started.append(copy)
         return copy
 
+    for arrival in arrivals:
+        arrival.wait()
     lane = lax.broadcasted_iota(jnp.int32, (LPD, ROWS), 1)
     line = lax.broadcasted_iota(jnp.int32, (LPD, ROWS), 0)
-    own = jnp.sum(jnp.where(lane == me.c * LPD + line, lrows[...], 0.0), axis=1, keepdims=True)
+    lrows = wide(lrows_in[...]).astype(F32)
+    own = jnp.sum(jnp.where(lane == me.c * LPD + line, lrows, 0.0), axis=1, keepdims=True)
     rows_at = lax.broadcasted_iota(jnp.int32, (LPD, 128), 1).astype(F32)
     pick = (own == rows_at).astype(F32).astype(BF16)
-    mine_cols = pl.ds(pl.multiple_of(me.v * 1024, 1024), 1024)
-    rows[me.z, me.xh, me.core, :, mine_cols] = jnp.dot(
-        pick, hidden[...], preferred_element_type=F32
-    ).astype(BF16)
+    rows[0, me.xh, me.core, me.xl, me.y] = jnp.dot(pick, hidden[...], preferred_element_type=F32).astype(BF16)
     picked_q = jnp.dot(pick, queries[...], preferred_element_type=F32).astype(BF16)
-    kvq[me.z, me.xh, me.core, 0:128, :] = keys[...]
-    kvq[me.z, me.xh, me.core, 128:256, :] = values[...]
     for head in range(8):
         kvq[me.z, me.xh, me.core, 256 + 8 * head : 264 + 8 * head, :] = picked_q[:, 128 * head : 128 * head + 128]
     greeted()
 
-    def block(k, off):
-        cols = pl.ds(pl.multiple_of(me.v_at(*off) * 1024, 1024), 1024)
-        return rows.at[pl.ds(2 * k, 2), me.xh_off(off[0]), me.core, :, cols]
-
-    own_block = rows.at[me.z, me.xh, me.core, :, mine_cols]
-    z_copies = [
-        go(own_block, own_block, z_s.at[d], z_r.at[d], me.dev(z=me.z_plus(d))) for d in range(1, NZ)
-    ]
+    def piece(k, at):
+        xh, xl, y = at
+        return rows.at[pl.ds(2 * k, 2), xh, me.core, xl, y]
+
+    z_copies = {}
+    for d in FAR_FIRST[:-1]:
+        back = NZ - d
+        z_copies[back] = go(
+            rows.at[0, me.xh, me.core, me.xl, me.y], rows.at[back, me.xh, me.core, me.xl, me.y],
+            z_s.at[d], z_r.at[back], me.dev(z=me.z_plus(d)),
+        )
     own_kvq = kvq.at[me.z, me.xh, me.core]
     k_x = go(own_kvq, own_kvq, k_s.at[0], k_r.at[0], me.dev(x_off=2))
-    for copy in z_copies:
-        copy.wait_recv()
-
-    a_copies, f_copies, kf_copies, ring = {}, [], [], {}
-
-    def spread(k, index, off, first):
-        here = block(k, off)
-        for step in range(first, 4):
-            slot = (1 << step) - 1 + index
-            a_copies[k, step, index] = go(
-                here, here, a_s.at[k, slot], a_r.at[k, slot], partner(me, *ORDERS[k][step])
+
+    a_copies, f_copies, kf_copies, ring = {}, {}, [], {}
+
+    def spread(k, step):
+        order = ORDERS[k]
+        for j, at in enumerate(pieces(me, order, step)):
+            here = piece(k, at)
+            for later in range(step + 1, 4):
+                a_copies.setdefault((k, later), []).append(
+                    go(
+                        here, here, a_s.at[k, later, 2 * step + 2 + j], a_r.at[k, later, 2 * step + 2 + j],
+                        partner(me, *order[later]),
+                    )
+                )
+            f_copies.setdefault(k, []).append(
+                go(here, here, f_s.at[k, 2 * step + 2 + j], f_r.at[k, 2 * step + 2 + j], mate)
             )
-        f_copies.append(go(here, here, f_s.at[k, index], f_r.at[k, index], mate))
-
-    def arrive(step, js):
-        for j in js:
-            for k, order in enumerate(ORDERS):
-                a_copies[k, step, j].wait_recv()
-                index = (1 << step) + j
-                spread(k, index, offsets(order, step + 1)[index], step + 1)
+
+    def place_tables():
+        spans = jnp.broadcast_to(stretch[...].astype(F32), (8, 64)).astype(BF16)
+
+        def spread_spans(slot, width):
+            hot = lax.broadcasted_iota(jnp.int32, (64, width), 0) == slot
+            return jnp.dot(spans, hot.astype(F32).astype(BF16), preferred_element_type=F32)[0:1]
+
+        at = lax.broadcasted_iota(jnp.int32, (1, NC * 128), 1)
+        base = spread_spans(lax.shift_right_logical(at, 6), NC * 128)
+        key_pos[...] = base * 64.0 + (at & 63).astype(F32)
+        at = lax.broadcasted_iota(jnp.int32, (1, NC * 64), 1)
+        owner = lax.shift_right_logical(at, 6)
+        hot = lax.broadcasted_iota(jnp.int32, (ROWS, NC * 64), 0) == owner * LPD + (at & 7)
+        local = jnp.dot(
+            jnp.broadcast_to(lrows, (8, ROWS)).astype(BF16), hot.astype(F32).astype(BF16), preferred_element_type=F32
+        )[0:1]
+        first, second = spread_spans(owner * 2, NC * 64), spread_spans(owner * 2 + 1, NC * 64)
+        query_pos[...] = jnp.where(local < 64.0, first * 64.0 + local, second * 64.0 + (local - 64.0))
+        for t in range(WIDTH // 128):
+            gain[:, 128 * t : 128 * t + 128] = gain_in[t : t + 1, :]
 
     def ring_step(step):
         lo, hi = (0, KVQ) if step < 4 else (0, 160)
@@ -214,35 +274,45 @@
         ring[step][1].wait_recv()
         ring_forward(2 * step if step < 4 else 7, me.z_plus(step))
 
-    for k in range(4):
-        spread(k, 0, (0, 0), 0)
-    arrive(0, range(1))
-    k_x.wait_recv()
-    ring_step(1)
-    ring_forward(0, me.z)
-    arrive(1, range(2))
-    arrive(2, range(4))
-    ring_wait(1)
-    ring_step(2)
-    arrive(3, range(4))
+    def prepare(d, _):
+        lines = pl.ds(pl.multiple_of(lax.rem(me.z + d, NZ) * 32, 32), 32)
+        square = jnp.zeros((32, 128), F32)
+        for v in range(NV):
+            cols = slice(1024 * v, 1024 * v + 1024)
+            x = rows[d, :, :, v // 4, v % 4].astype(F32).reshape(32, 1024)
+            y[lines, cols] = (x * gain[:, cols]).astype(BF16)
+            sq = x * x
+            for t in range(8):
+                square = square + sq[:, 128 * t : 128 * t + 128]
+        inv = lax.rsqrt(jnp.sum(square, axis=1, keepdims=True) * (1.0 / WIDTH) + EPS)
+        rms_col[lines, :] = jnp.broadcast_to(inv, (32, 128))
+        return 0
+
+    place_tables()
+    for kind, which in GATHER:
+        if kind == "z":
+            for d in (2 * which, 2 * which + 1):
+                if d:
+                    z_copies[d].wait_recv()
+            spread(which, -1)
+        elif kind == "r":
+            if which == 1:
+                k_x.wait_recv()
+                ring_forward(0, me.z)
+            else:
+                ring_wait(which - 1)
+            ring_step(which)
+        elif kind == "p":
+            for copy in f_copies[which]:
+                copy.wait_recv()
+            lax.fori_loop(2 * which, 2 * which + 2, prepare, 0)
+        else:
+            for copy in a_copies[kind, which]:
+                copy.wait_recv()
+            spread(kind, which)
     ring_wait(2)
     ring_step(3)
-    arrive(3, range(4, 8))
-    for copy in f_copies:
-        copy.wait_recv()
-
-    def prepare(j, square):
-        cols = pl.ds(pl.multiple_of(j * 1024, 1024), 1024)
-        x = rows[:, :, :, :, cols].astype(F32).reshape(ROWS, 1024)
-        y[:, cols] = (x * gain[:, cols]).astype(BF16)
-        sq = x * x
-        for t in range(8):
-            square = square + sq[:, 128 * t : 128 * t + 128]
-        return square
-
-    square = lax.fori_loop(0, 8, prepare, jnp.zeros((ROWS, 128), F32))
-    inv_col = lax.rsqrt(jnp.sum(square, axis=1, keepdims=True) * (1.0 / WIDTH) + EPS)
-    rms_col[...] = jnp.broadcast_to(inv_col, (ROWS, 128))
+
     inv_row = jnp.transpose(rms_col[...])[0:1, :]
 
     logits[PAD - 48 : PAD, :] = jnp.zeros((48, ROWS), F32)
@@ -253,14 +323,14 @@
             (((1,), (1,)), ((), ())), preferred_element_type=F32,
         )
         logits[0:VOC, :] = term if j == 0 else logits[0:VOC, :] + term
-        if j == 3:
+        if j == 6:
             ring_wait(3)
             ring_step(4)
 
     ids = lax.broadcasted_iota(jnp.int32, (PAD, ROWS), 0)
     real = ids < VOC
     first_id = (me.v * NC + me.c) * VOC
-    is_target = ((ids + first_id) == targets[...]) & real
+    is_target = ((ids + first_id) == wide(targets_in[...])) & real
     value = jnp.where(real, logits[...] * inv_row, FILL)
     logits[...] = value
     top = jnp.max(value, axis=0, keepdims=True)
@@ -279,6 +349,13 @@
         waits.append(
             go(st1.at[slot1], st1.at[slot1], s1_s.at[i], s1_r.at[2 * d + o], me.dev(z=me.z_plus(d), core_off=o))
         )
+    for copy in waits:
+        copy.wait_recv()
+    slot2 = (me.xh * 2 + me.xl) * 4 + me.y
+    st2[slot2] = merge(st1[...])
+    waits = []
+    for i, (ox, oy) in enumerate(group2):
+        waits.append(go(st2.at[slot2], st2.at[slot2], s2_s.at[i], s2_r.at[4 * ox + oy], me.dev(ox, oy)))
     ring_wait(4)
     for copy in kf_copies:
         copy.wait_recv()
@@ -290,13 +367,6 @@
     lane = lax.broadcasted_iota(jnp.int32, (64, NC * 64), 1)
     line = lax.broadcasted_iota(jnp.int32, (64, NC * 64), 0)
     query_col = jnp.sum(jnp.where(lane == me.c * 64 + line, query_pos[...], 0.0), axis=1, keepdims=True)
-    for copy in waits:
-        copy.wait_recv()
-    slot2 = (me.xh * 2 + me.xl) * 4 + me.y
-    st2[slot2] = merge(st1[...])
-    waits = []
-    for i, (ox, oy) in enumerate(group2):
-        waits.append(go(st2.at[slot2], st2.at[slot2], s2_s.at[i], s2_r.at[4 * ox + oy], me.dev(ox, oy)))
     scores = lax.dot_general(q_own, k_all[...], (((1,), (1,)), ((), ())), preferred_element_type=F32)
     seen = key_pos[...] <= query_col
     masked = jnp.where(seen, scores * SCALE, FILL)
@@ -319,87 +389,91 @@
         return jnp.dot(grad_t[:, 0:VOC], weight[:, cols], preferred_element_type=F32).reshape(NV, 32, 256)
 
     c_copies = {}
-    z_order = (0, 2, 4, 6, 1, 3, 5, 7)
-    for z in z_order:
-
-        def other(xh, _, z=z):
+
+    def give(d):
+        z = me.z_plus(d)
+
+        def other(xh, _):
             cs[z, xh] = chunk(z, xh, 1 - me.core).astype(BF16)
             return 0
 
         lax.fori_loop(0, 2, other, 0)
-        c_copies[z] = go(cs.at[z], cr.at[z], c_s.at[z], c_r.at[z], mate)
+        c_copies[d] = go(cs.at[z], cr.at[z], c_s.at[d], c_r.at[d], mate)
+
+    def keep_own(d):
+        z = me.z_plus(d)
+
+        def mine(xh, _):
+            acc[z, xh] = chunk(z, xh, me.core)
+            return 0
+
+        lax.fori_loop(0, 2, mine, 0)
 
     sends, recvs = (sb1, sb2, sb3, sb4), (rb1, rb2, rb3, rb4)
     moving = {}
 
-    def at(z, off):
-        return (z, me.xh_off(off[0]), me.v_at(*off))
-
-    def halve(z, step):
-        back = ORDERS[z // 2]
+    def at(d, off):
+        return (me.z_plus(d), me.xh_off(off[0]), me.v_at(*off))
+
+    def halve(d, step):
+        back = ORDERS[COLOUR[d]]
         axis, mask = back[3 - step]
         keep, before = offsets(back, 3 - step), offsets(back, 4 - step)
         for off in before:
-            here = at(z, off)
+            here = at(d, off)
             if step == 0:
                 extra = cr[here].astype(F32)
             else:
-                extra = recvs[step - 1][z, before.index(off)].astype(F32)
+                extra = recvs[step - 1][d, before.index(off)].astype(F32)
             summed = acc[here] + extra
             away = (off[0] ^ mask, off[1]) if axis == "x" else (off[0], off[1] ^ mask)
             if away in keep:
-                sends[step][z, keep.index(away)] = summed.astype(BF16)
+                sends[step][d, keep.index(away)] = summed.astype(BF16)
             else:
                 acc[here] = summed
-        moving[z, step] = go(
-            sends[step].at[z], recvs[step].at[z], x_s.at[z, step], x_r.at[z, step], partner(me, axis, mask)
+        moving[d, step] = go(
+            sends[step].at[d], recvs[step].at[d], x_s.at[d, step], x_r.at[d, step], partner(me, axis, mask)
         )
 
-    for z in z_order:
-
-        def mine(xh, _, z=z):
-            acc[z, xh] = chunk(z, xh, me.core)
-            return 0
-
-        lax.fori_loop(0, 2, mine, 0)
-        c_copies[z].wait_recv()
-        halve(z, 0)
-    for step in range(1, 4):
-        for z in z_order:
-            moving[z, step - 1].wait_recv()
-            halve(z, step)
-
-    def z_copy(z, src):
-        return pltpu.make_async_remote_copy(
-            src_ref=zs.at[z], dst_ref=zr.at[src], send_sem=t_s.at[z], recv_sem=t_r.at[src],
-            device_id=me.dev(z=jnp.int32(z)), device_id_type=MESH,
-        )
-
-    for z in z_order:
-        moving[z, 3].wait_recv()
-        zs[z] = (acc[at(z, (0, 0))] + rb4[z, 0].astype(F32)).astype(BF16)
-
-        @pl.when(me.z != z)
-        def _(z=z):
-            z_copy(z, me.z).start()
+    z_copies = []
+    lag = 4
+    give(FAR_FIRST[0])
+    for i in range(NZ + 4 * lag):
+        if i + 1 < NZ:
+            give(FAR_FIRST[i + 1])
+        if i < NZ:
+            d = FAR_FIRST[i]
+            keep_own(d)
+            c_copies[d].wait_recv()
+            halve(d, 0)
+        for step in range(1, 5):
+            if not 0 <= i - lag * step < NZ:
+                continue
+            d = FAR_FIRST[i - lag * step]
+            moving[d, step - 1].wait_recv()
+            if step < 4:
+                halve(d, step)
+                continue
+            zs[d] = (acc[at(d, (0, 0))] + rb4[d, 0].astype(F32)).astype(BF16)
+            if d:
+                z_copies.append(go(zs.at[d], zr.at[me.z], t_s.at[d], t_r.at[d], me.dev(z=me.z_plus(d))))
+            else:
+                zr[me.z] = zs[d]
 
     loss[...] = jnp.broadcast_to(jnp.mean(log_total - hit, axis=1, keepdims=True), (8, 128))
     inner_col[...] = column((wide(final[4:6] / final[2:4]) - hit) * (GRAD_WEIGHT / WIDTH))
     k_own = kvq[me.z, me.xh, me.core, 0:128, :]
     v_own = kvq[me.z, me.xh, me.core, 128:256, :]
     s2[...] = lax.dot_general(k_own, q_all[...], (((1,), (1,)), ((), ())), preferred_element_type=F32)
-    zr[me.z] = zs[me.z]
-    for z in range(NZ):
-
-        @pl.when(me.z != z)
-        def _(z=z):
-            z_copy(z, z).wait_recv()
-
+    for copy in z_copies:
+        copy.wait_recv()
     normed_grad = jnp.sum(zr[...].astype(F32), axis=0)
     cols = pl.ds(pl.multiple_of(me.c * 256, 256), 256)
     lines = pl.ds(pl.multiple_of(me.v * 32, 32), 32)
     inv = rms_col[lines, 0:1]
-    picked = rows[me.v, :, :, :, cols].astype(F32).reshape(32, 256)
+    inside = pl.ds(pl.multiple_of(lax.rem(me.c, 4) * 256, 256), 256)
+    apart = lax.rem(me.v - me.z + NZ, NZ)
+    picked = rows[apart, :, :, lax.div(me.z, 4), lax.rem(me.z, 4), :, inside].astype(F32).reshape(32, 256)
     out = inv * (normed_grad * gain[:, cols] - picked * (inv * inner_col[lines, 0:1]))
     resid[me.v] = out.astype(BF16)
     v_copies = []
@@ -413,58 +487,78 @@
     for copy in v_copies:
         copy.wait_recv()
 
+    out_load.wait()
     wide_part = lax.dot_general(
         resid[...].reshape(ROWS, 256), out_weight[...], (((1,), (1,)), ((), ())), preferred_element_type=F32
     )
     for h in range(8):
         part[:, :, :, 8 * h : 8 * h + 8, :] = wide_part[:, 128 * h : 128 * h + 128].reshape(NZ, 2, 2, LPD, HEAD)
-    pc[...] = part[:, :, 1 - me.core].astype(BF16)
-    pc_copy = go(pc, pr, pc_s, pc_r, mate)
+    pc_copies = {}
+    for d in FAR_FIRST:
+        z = me.z_plus(d)
+        pc[z] = part[z, :, 1 - me.core].astype(BF16)
+        pc_copies[d] = go(pc.at[z], pr.at[z], pc_s.at[d], pc_r.at[d], mate)
+    x_copies, r_copies = {}, []
+    for d in FAR_FIRST:
+        z = me.z_plus(d)
+        pc_copies[d].wait_recv()
+        there = 1 - me.xh
+        rs[z] = (part[z, there, me.core] + pr[z, there].astype(F32)).astype(BF16)
+        x_copies[d] = go(rs.at[z], rx.at[z], rx_s.at[d], rx_r.at[d], me.dev(x_off=2))
+    for d in FAR_FIRST:
+        z = me.z_plus(d)
+        x_copies[d].wait_recv()
+        mine = part[z, me.xh, me.core] + pr[z, me.xh].astype(F32) + rx[z].astype(F32)
+        if d:
+            rz[z] = mine.astype(BF16)
+            r_copies.append(go(rz.at[z], rr.at[me.z], r_s.at[d], r_r.at[d], me.dev(z=z)))
+        else:
+            rr[me.z] = mine.astype(BF16)
     resid_t[...] = jnp.transpose(resid[...].astype(F32).reshape(ROWS, 256)).astype(BF16)
-    pc_copy.wait_recv()
-    rs[...] = (part[:, :, me.core] + pr[...].astype(F32)).astype(BF16)
-    r_copies = []
-    for i, (d, o) in enumerate(peers):
-        z, xh = me.z_plus(d), me.xh_off(o)
-        r_copies.append(go(rs.at[z, xh], rr.at[me.z, me.xh], r_s.at[i], r_r.at[i], me.dev(z=z, x_off=o)))
-    rr[me.z, me.xh] = rs[me.z, me.xh]
     for copy in r_copies:
         copy.wait_recv()
-    grad_own = jnp.sum(rr[...].astype(F32), axis=(0, 1)).astype(BF16)
+    grad_own = jnp.sum(rr[...].astype(F32), axis=0).astype(BF16)
     grads[me.z, me.xh, me.core] = grad_own
+    own_g, own_e = grads.at[me.z, me.xh, me.core], extras.at[me.z, me.xh, me.core]
+
+    def hand_out(own, send, recv):
+        return {d: go(own, own, send.at[d], recv.at[d], me.dev(z=me.z_plus(d))) for d in FAR_FIRST[:-1]}
+
+    g_copies = hand_out(own_g, g_s, g_r)
     delta = jnp.sum(grad_own.astype(F32) * attn_out, axis=1, keepdims=True)
     lane = lax.broadcasted_iota(jnp.int32, (64, 128), 1)
     square_tile[...] = jnp.zeros((128, 128), F32)
     square_tile[0:64, :] = jnp.where(lane == 0, delta, jnp.where(lane == 1, row_log_total, 0.0))
     extras[me.z, me.xh, me.core] = jnp.transpose(square_tile[...])[0:8, :]
-    own_g, own_e = grads.at[me.z, me.xh, me.core], extras.at[me.z, me.xh, me.core]
-    g_copies = []
-    for i, (d, o) in enumerate(peers):
-        device = me.dev(z=me.z_plus(d), x_off=o)
-        g_copies.append(
-            (
-                go(own_g, own_g, g_s.at[i], g_r.at[i], device),
-                go(own_e, own_e, e_s.at[i], e_r.at[i], device),
-                d,
-                o,
-            )
-        )
-    forwards = [
-        go(own_g, own_g, fg_s.at[15], fg_r.at[15], mate),
-        go(own_e, own_e, fe_s.at[15], fe_r.at[15], mate),
-    ]
+    e_copies = hand_out(own_e, e_s, e_r)
+    side = me.dev(x_off=2)
+    forwards, sides = [], {}
+
+    def hand_on(d, xh, slot):
+        here = grads.at[me.z_plus(-d), xh, me.core]
+        if not slot:
+            sides[d] = go(here, here, gx_s.at[d], gx_r.at[d], side)
+        forwards.append(go(here, here, fg_s.at[slot, d], fg_r.at[slot, d], mate))
+
+    hand_on(0, me.xh, 0)
     prob_grad = lax.dot_general(grad_own, v_all[...], (((1,), (1,)), ((), ())), preferred_element_type=F32)
     score_grad = (probs[...] * (prob_grad - delta)).astype(BF16)
     query_grad = jnp.dot(score_grad, k_all[...], preferred_element_type=F32) * SCALE
     for h in range(8):
         dq[:, 128 * h : 128 * h + 128] = query_grad[8 * h : 8 * h + 8, :].astype(BF16)
-    for i, (g_copy, e_copy, d, o) in enumerate(g_copies):
-        z, xh = me.z_plus(-d), me.xh_off(o)
-        g_copy.wait_recv()
-        e_copy.wait_recv()
-        here_g, here_e = grads.at[z, xh, me.core], extras.at[z, xh, me.core]
-        forwards.append(go(here_g, here_g, fg_s.at[i], fg_r.at[i], mate))
-        forwards.append(go(here_e, here_e, fe_s.at[i], fe_r.at[i], mate))
+    for d in NEAR_FIRST[1:]:
+        g_copies[d].wait_recv()
+        hand_on(d, me.xh, 0)
+    for copy in e_copies.values():
+        copy.wait_recv()
+    line_e = extras.at[:, me.xh, me.core]
+    e_side = go(line_e, line_e, ex_s, ex_r, side)
+    for d in NEAR_FIRST:
+        sides[d].wait_recv()
+        hand_on(d, 1 - me.xh, 1)
+    e_side.wait_recv()
+    all_e = extras.at[:, :, me.core]
+    forwards.append(go(all_e, all_e, fe_s, fe_r, mate))
     own_key_pos = key_pos[:, pl.ds(pl.multiple_of(me.c * 128, 128), 128)]
     lane = lax.broadcasted_iota(jnp.int32, (128, 128), 1)
     line = lax.broadcasted_iota(jnp.int32, (128, 128), 0)
@@ -483,11 +577,6 @@
     dk[...] = (jnp.dot(score_grad2, q_all[...], preferred_element_type=F32) * SCALE).astype(BF16)
     for copy in started:
         copy.wait_send()
-    for z in range(NZ):
-
-        @pl.when(me.z != z)
-        def _(z=z):
-            z_copy(z, me.z).wait_send()
 
 
 def step(*operands):
@@ -504,11 +593,11 @@
             jax.ShapeDtypeStruct((128, HEAD), BF16),
             jax.ShapeDtypeStruct((128, HEAD), BF16),
         ),
-        in_specs=[vmem] * 10 + [pl.BlockSpec(memory_space=pl.ANY)],
+        in_specs=[pl.BlockSpec(memory_space=pl.ANY)] * 10,
         out_specs=(vmem,) * 5,
         scratch_shapes=[
             scratch((VOC, WIDTH), BF16),
-            scratch((NZ, 2, 2, LPD, WIDTH), BF16),
+            scratch((NZ, 2, 2, 2, 4, LPD, 1024), BF16),
             scratch((ROWS, WIDTH), BF16),
             scratch((NZ, 2, 2, KVQ, HEAD), BF16),
             scratch((PAD, ROWS), F32),
@@ -530,17 +619,28 @@
             scratch((NC * 64, HEAD), BF16),
             scratch((64, NC * 128), F32),
             scratch((NZ, 2, 2, 64, HEAD), F32),
-            *[scratch((NZ, 2, 64, HEAD), BF16)] * 4,
+            *[scratch((NZ, 2, 64, HEAD), BF16)] * 2,
+            *[scratch((NZ, 64, HEAD), BF16)] * 4,
             scratch((NZ, 2, 2, 64, HEAD), BF16),
             scratch((NZ, 2, 2, 8, 128), F32),
             scratch((128, 128), F32),
             scratch((128, NC * 64), F32),
-            dma((8,)), dma((NZ,)), dma((NZ,)), dma((4, 15)), dma((4, 15)), dma((4, 16)), dma((4, 16)),
+            scratch((1, NC * 128), F32),
+            scratch((1, NC * 64), F32),
+            scratch((1, WIDTH), F32),
+            scratch((1024, 256), BF16),
+            scratch((128, 1024), BF16),
+            scratch((128, 1024), BF16),
+            scratch((2, 128), jnp.int32),
+            scratch((2, 128), jnp.int32),
+            scratch((64, 128), F32),
+            scratch((1, 64), jnp.int32),
+            dma((8,)), dma, dma((8,)), dma((NZ,)), dma((NZ,)),
+            dma((4, 4, 8)), dma((4, 4, 8)), dma((4, 10)), dma((4, 10)),
             dma((9,)), dma((9,)), dma((8,)), dma((8,)),
             dma((16,)), dma((16,)), dma((16,)), dma((16,)), dma((NZ,)), dma((NZ,)),
             dma((NZ, 4)), dma((NZ, 4)), dma((NZ,)), dma((NZ,)), dma((7,)), dma((7,)),
-            dma, dma, dma((15,)), dma((15,)), dma((15,)), dma((15,)), dma((15,)), dma((15,)),
-            dma((16,)), dma((16,)), dma((16,)), dma((16,)),
+            *[dma((NZ,))] * 12, dma((2, NZ)), dma((2, NZ)), dma, dma, dma, dma,
         ],
         compiler_params=pltpu.CompilerParams(
             collective_id=0, has_side_effects=True, vmem_limit_bytes=61 * 1024 * 1024
@@ -581,22 +681,15 @@
     attention_values,
     output_weight,
 ):
-    spans = stretch_of_slot.reshape(NC, 2)
-    local = loss_rows.reshape(NC, LPD)
-    place = jnp.where(local < 64, spans[:, 0:1], spans[:, 1:2]) * 64 + lax.rem(local, 64)
-    query_pos = jnp.broadcast_to(place[:, None, :], (NC, 8, LPD)).reshape(1, NC * 64).astype(F32)
-    key_pos = stretch_of_slot[:, None] * 64 + lax.broadcasted_iota(jnp.int32, (64, 64), 1)
-    key_pos = key_pos.reshape(1, 4096).astype(F32)
     loss, resid_t, dq, dk, dv = step(
         hidden,
         queries,
         key_states,
         attention_values,
-        loss_rows.astype(F32).reshape(1, ROWS),
-        targets.reshape(1, ROWS),
-        norm_gain.reshape(1, WIDTH),
-        key_pos,
-        query_pos,
+        loss_rows.reshape(2, 128),
+        targets.reshape(2, 128),
+        norm_gain.reshape(64, 128),
+        stretch_of_slot.reshape(1, 64),
         output_weight,
         head_weight,
     )

time: 127 us -> 119 us (0.937)
  local copies, waits for them, and re-layouts: 3.12 us -> 0 us
  Pallas kernels: 121 us -> 118 us
  other arithmetic: 2.06 us -> 0 us
    pallas_call x1, Pallas kernels: 119 us -> 116 us  [step(): pl.pallas_call(step_kernel, out_shape=(jax.ShapeDtypeStruct((8, 128), F32...]
    reshape x2 -> x0, local copies, waits for them, and re-layouts: 1.51 us -> none  [the longest x1 0.76 us: per_device(): spans = stretch_of_slot.reshape(NC, 2)]
    convert_element_type x2 -> x0, local copies, waits for them, and re-layouts: 1.42 us -> none  [the longest x1 0.72 us: per_device(): jnp.broadcast_to(place[:, None, :], (NC, 8, LPD)).reshape(1, NC * 64)]
    convert_element_type x3 -> x0, other arithmetic: 1.4 us -> none  [the longest x1 1.24 us: per_device(): loss_rows.astype(F32).reshape(1, ROWS)]
where the time goes in v3:
time: 119 us
  Pallas kernels  118 us (99%)
    pallas_call x1, Pallas kernels, step(): pl.pallas_call(step_kernel, out_shape=(jax.ShapeDtypeStruct((8, 128), F32...  116 us

profile of v3, /device:TPU:1, one launch (start us, length us, event | category | flops | bytes accessed | tf_op | source)
XLA Modules:
  0.0 118.8 jit_solution(12500835039545259361)
XLA Ops:
  0.6 116.4 %step.1 = (f32[8,128]{1,0:T(8,128)}, bf16[256,256]{1,0:T(8,128)(2,1)}, bf16[8,1024]{1,0:T(8,128)(2,1)}, bf16[128,128]{1,0:T(8,128)(2,1)}, bf16[128,128]{1,0:T(8,128)(2,1)}) custom-call(bf16[128,1024]{1,0:T(8,128)(2,1)} %hidden_hbm.1, bf16[128,1024]{1,0:T(8,128)(2,1)} %queries_hbm.1, bf16[128,128]{1,0:T(8,128)(2,1)} %keys_hbm.1, bf16[128,128]{1,0:T(8,128)(2,1)} %values_hbm.1, ...), custom_call_target="tpu_custom_call" | custom-call | tf_op jit(solution)/shard_map/step/pallas_call | solution.py:587
  117.1 1.6 %emit.1 = (f32[1,1]{1,0:T(1,128)}, bf16[256,256]{1,0:T(8,128)(2,1)}, bf16[8,1024]{1,0:T(8,128)(2,1)}, bf16[128,128]{1,0:T(8,128)(2,1)}, bf16[128,128]{1,0:T(8,128)(2,1)}) custom-call(f32[8,128]{1,0:T(8,128)} %get-tuple-element.15.loss, bf16[256,256]{1,0:T(8,128)(2,1)} %get-tuple-element.16.resid_t, bf16[8,1024]{1,0:T(8,128)(2,1)} %get-tuple-element.17.dq, ...), custom_call_target="tpu_custom_call" | custom-call | tf_op jit(solution)/shard_map/emit/pallas_call | solution.py:662

commit v4 on v3

--- a/solution.py
+++ b/solution.py
@@ -148,7 +148,7 @@
 def step_kernel(
     hidden_hbm, queries_hbm, keys_hbm, values_hbm, lrows_hbm, targets_hbm, gain_hbm, stretch_hbm, out_hbm, weight_hbm,
     loss, resid_t, dq, dk, dv,
-    weight, rows, y, kvq, logits, grad_t, rms_col, inner_col, st1, st2, cs, cr, acc,
+    weight, rows, y, kvq, logits, logits_t, target_t, grad_t, rms_col, inner_col, st1, st2, cs, cr, acc,
     sb1, sb2, sb3, sb4, rb1, rb2, rb3, rb4, zs, zr, resid,
     k_all, v_all, q_all, probs, part, pc, pr, rs, rx, rz, rr, grads, extras, square_tile, s2,
     key_pos, query_pos, gain, out_weight, hidden, queries, lrows_in, targets_in, gain_in, stretch, w_sem, o_sem, i_sem, z_s, z_r, a_s, a_r, f_s, f_r, k_s, k_r, kf_s, kf_r, s1_s, s1_r, s2_s, s2_r,
@@ -188,6 +188,11 @@
 
     for arrival in arrivals:
         arrival.wait()
+    def drain():
+        for copy in started:
+            copy.wait_send()
+        started.clear()
+
     lane = lax.broadcasted_iota(jnp.int32, (LPD, ROWS), 1)
     line = lax.broadcasted_iota(jnp.int32, (LPD, ROWS), 0)
     lrows = wide(lrows_in[...]).astype(F32)
@@ -227,9 +232,9 @@
                         partner(me, *order[later]),
                     )
                 )
-            f_copies.setdefault(k, []).append(
-                go(here, here, f_s.at[k, 2 * step + 2 + j], f_r.at[k, 2 * step + 2 + j], mate)
-            )
+        if step == 3:
+            whole = rows.at[pl.ds(2 * k, 2), :, me.core]
+            f_copies[k] = [go(whole, whole, f_s.at[k, 0], f_r.at[k, 0], mate)]
 
     def place_tables():
         spans = jnp.broadcast_to(stretch[...].astype(F32), (8, 64)).astype(BF16)
@@ -349,6 +354,11 @@
         waits.append(
             go(st1.at[slot1], st1.at[slot1], s1_s.at[i], s1_r.at[2 * d + o], me.dev(z=me.z_plus(d), core_off=o))
         )
+    logits_t[...] = jnp.transpose(logits[...])
+    across = lax.broadcasted_iota(jnp.int32, (ROWS, PAD), 1)
+    wanted = column(wide(targets_in[...]).astype(F32))[:, 0:1]
+    hit_here = ((across + first_id).astype(F32) == wanted) & (across < VOC)
+    target_t[...] = hit_here.astype(F32).astype(BF16)
     for copy in waits:
         copy.wait_recv()
     slot2 = (me.xh * 2 + me.xl) * 4 + me.y
@@ -376,13 +386,14 @@
     probs[...] = raw / total
     row_log_total = top + jnp.log(total)
 
+    drain()
     for copy in waits:
         copy.wait_recv()
     final = merge(st2[...])
     log_total = wide(final[0:2] + jnp.log(final[2:4]))
     hit = wide(final[6:8])
-    grad = GRAD_WEIGHT * (jnp.exp(logits[...] - log_total) - is_target.astype(F32))
-    grad_t[...] = jnp.transpose(grad).astype(BF16)
+    grad = jnp.exp(logits_t[...] - column(log_total)[:, 0:1]) - target_t[...].astype(F32)
+    grad_t[...] = (GRAD_WEIGHT * grad).astype(BF16)
 
     def chunk(z, xh, core):
         cols = pl.ds(pl.multiple_of((z * 4 + xh * 2 + core) * 256, 256), 256)
@@ -415,24 +426,26 @@
     def at(d, off):
         return (me.z_plus(d), me.xh_off(off[0]), me.v_at(*off))
 
-    def halve(d, step):
-        back = ORDERS[COLOUR[d]]
+    def halve(d, part_of, step):
+        back = ORDERS[(COLOUR[d] + 2 * part_of) % 4]
         axis, mask = back[3 - step]
         keep, before = offsets(back, 3 - step), offsets(back, 4 - step)
+        lines = slice(16 * part_of, 16 * part_of + 16)
         for off in before:
-            here = at(d, off)
+            here = at(d, off) + (lines,)
             if step == 0:
                 extra = cr[here].astype(F32)
             else:
-                extra = recvs[step - 1][d, before.index(off)].astype(F32)
+                extra = recvs[step - 1][d, part_of, before.index(off)].astype(F32)
             summed = acc[here] + extra
             away = (off[0] ^ mask, off[1]) if axis == "x" else (off[0], off[1] ^ mask)
             if away in keep:
-                sends[step][d, keep.index(away)] = summed.astype(BF16)
+                sends[step][d, part_of, keep.index(away)] = summed.astype(BF16)
             else:
                 acc[here] = summed
-        moving[d, step] = go(
-            sends[step].at[d], recvs[step].at[d], x_s.at[d, step], x_r.at[d, step], partner(me, axis, mask)
+        moving[d, part_of, step] = go(
+            sends[step].at[d, part_of], recvs[step].at[d, part_of],
+            x_s.at[d, part_of, step], x_r.at[d, part_of, step], partner(me, axis, mask),
         )
 
     z_copies = []
@@ -445,16 +458,21 @@
             d = FAR_FIRST[i]
             keep_own(d)
             c_copies[d].wait_recv()
-            halve(d, 0)
+            for part_of in range(2):
+                halve(d, part_of, 0)
         for step in range(1, 5):
             if not 0 <= i - lag * step < NZ:
                 continue
             d = FAR_FIRST[i - lag * step]
-            moving[d, step - 1].wait_recv()
+            for part_of in range(2):
+                moving[d, part_of, step - 1].wait_recv()
+                if step < 4:
+                    halve(d, part_of, step)
+                else:
+                    lines = slice(16 * part_of, 16 * part_of + 16)
+                    zs[d, lines] = (acc[at(d, (0, 0)) + (lines,)] + rb4[d, part_of, 0].astype(F32)).astype(BF16)
             if step < 4:
-                halve(d, step)
                 continue
-            zs[d] = (acc[at(d, (0, 0))] + rb4[d, 0].astype(F32)).astype(BF16)
             if d:
                 z_copies.append(go(zs.at[d], zr.at[me.z], t_s.at[d], t_r.at[d], me.dev(z=me.z_plus(d))))
             else:
@@ -484,6 +502,7 @@
     attn_out = jnp.dot(high, v_all[...], preferred_element_type=F32) + jnp.dot(
         low, v_all[...], preferred_element_type=F32
     )
+    drain()
     for copy in v_copies:
         copy.wait_recv()
 
@@ -515,6 +534,7 @@
         else:
             rr[me.z] = mine.astype(BF16)
     resid_t[...] = jnp.transpose(resid[...].astype(F32).reshape(ROWS, 256)).astype(BF16)
+    drain()
     for copy in r_copies:
         copy.wait_recv()
     grad_own = jnp.sum(rr[...].astype(F32), axis=0).astype(BF16)
@@ -564,6 +584,7 @@
     line = lax.broadcasted_iota(jnp.int32, (128, 128), 0)
     key_col = jnp.sum(jnp.where(lane == line, own_key_pos, 0.0), axis=1, keepdims=True)
     seen2 = key_col <= query_pos[...]
+    drain()
     for copy in forwards:
         copy.wait_recv()
     grads_all = grads[...].reshape(NC * 64, HEAD)
@@ -575,8 +596,6 @@
     prob_grad2 = lax.dot_general(v_own, grads_all, (((1,), (1,)), ((), ())), preferred_element_type=F32)
     score_grad2 = (probs2 * (prob_grad2 - delta_all)).astype(BF16)
     dk[...] = (jnp.dot(score_grad2, q_all[...], preferred_element_type=F32) * SCALE).astype(BF16)
-    for copy in started:
-        copy.wait_send()
 
 
 def step(*operands):
@@ -601,6 +620,8 @@
             scratch((ROWS, WIDTH), BF16),
             scratch((NZ, 2, 2, KVQ, HEAD), BF16),
             scratch((PAD, ROWS), F32),
+            scratch((ROWS, PAD), F32),
+            scratch((ROWS, PAD), BF16),
             scratch((ROWS, PAD), BF16),
             scratch((ROWS, 128), F32),
             scratch((ROWS, 128), F32),
@@ -609,8 +630,8 @@
             scratch((NZ, 2, NV, 32, 256), BF16),
             scratch((NZ, 2, NV, 32, 256), BF16),
             scratch((NZ, 2, NV, 32, 256), F32),
-            *[scratch((NZ, n, 32, 256), BF16) for n in halves],
-            *[scratch((NZ, n, 32, 256), BF16) for n in halves],
+            *[scratch((NZ, 2, n, 16, 256), BF16) for n in halves],
+            *[scratch((NZ, 2, n, 16, 256), BF16) for n in halves],
             scratch((NZ, 32, 256), BF16),
             scratch((NZ, 32, 256), BF16),
             scratch((NV, 32, 256), BF16),
@@ -639,7 +660,7 @@
             dma((4, 4, 8)), dma((4, 4, 8)), dma((4, 10)), dma((4, 10)),
             dma((9,)), dma((9,)), dma((8,)), dma((8,)),
             dma((16,)), dma((16,)), dma((16,)), dma((16,)), dma((NZ,)), dma((NZ,)),
-            dma((NZ, 4)), dma((NZ, 4)), dma((NZ,)), dma((NZ,)), dma((7,)), dma((7,)),
+            dma((NZ, 2, 4)), dma((NZ, 2, 4)), dma((NZ,)), dma((NZ,)), dma((7,)), dma((7,)),
             *[dma((NZ,))] * 12, dma((2, NZ)), dma((2, NZ)), dma, dma, dma, dma,
         ],
         compiler_params=pltpu.CompilerParams(

time: 119 us -> 118 us (level)
  no operation moved by 1% of the time
where the time goes in v4:
time: 118 us
  Pallas kernels  117 us (99%)
    pallas_call x1, Pallas kernels, step(): pl.pallas_call(step_kernel, out_shape=(jax.ShapeDtypeStruct((8, 128), F32...  115 us

profile of v4, /device:TPU:1, one launch (start us, length us, event | category | flops | bytes accessed | tf_op | source)
XLA Modules:
  0.0 117.8 jit_solution(8313131551209356612)
XLA Ops:
  0.6 115.4 %step.1 = (f32[8,128]{1,0:T(8,128)}, bf16[256,256]{1,0:T(8,128)(2,1)}, bf16[8,1024]{1,0:T(8,128)(2,1)}, bf16[128,128]{1,0:T(8,128)(2,1)}, bf16[128,128]{1,0:T(8,128)(2,1)}) custom-call(bf16[128,1024]{1,0:T(8,128)(2,1)} %hidden_hbm.1, bf16[128,1024]{1,0:T(8,128)(2,1)} %queries_hbm.1, bf16[128,128]{1,0:T(8,128)(2,1)} %keys_hbm.1, bf16[128,128]{1,0:T(8,128)(2,1)} %values_hbm.1, ...), custom_call_target="tpu_custom_call" | custom-call | tf_op jit(solution)/shard_map/step/pallas_call | solution.py:606
  116.1 1.6 %emit.1 = (f32[1,1]{1,0:T(1,128)}, bf16[256,256]{1,0:T(8,128)(2,1)}, bf16[8,1024]{1,0:T(8,128)(2,1)}, bf16[128,128]{1,0:T(8,128)(2,1)}, bf16[128,128]{1,0:T(8,128)(2,1)}) custom-call(f32[8,128]{1,0:T(8,128)} %get-tuple-element.15.loss, bf16[256,256]{1,0:T(8,128)(2,1)} %get-tuple-element.16.resid_t, bf16[8,1024]{1,0:T(8,128)(2,1)} %get-tuple-element.17.dq, ...), custom_call_target="tpu_custom_call" | custom-call | tf_op jit(solution)/shard_map/emit/pallas_call | solution.py:683
